TPU v7x, 512 devices: a whole 4x8x8 slice. The times are simulated.
512 devices in a mesh: ctx: 64 (over y, z), head: 8 (over x, core).
Axes of the slice: x: 4, y: 8, z: 8, core: 2. Of those that a mesh axis runs over, the one named last changes fastest.
Arguments:
- projected: bfloat16 [16384, 12288], P(('ctx', 'head')), may hold values from -6 to 6
- gate_logits: bfloat16 [16384, 64], P(('ctx', 'head')), as said below
- conv_weight: bfloat16 [4, 8192], P(None, 'head'), may hold values from -3 to 3
- decay_log: float32 [32], P('head'), as said below
- step_bias: float32 [32], P('head'), may hold values from -1 to 1
- norm_gain: float32 [128], replicated, may hold values from 0.1 to 1.9
Outputs:
- gated: bfloat16 [16384, 4096], P(('ctx', 'head'))
Inputs may be any that keep to these rules, and one draw needn't show every extreme that they name: `decay_log`: logarithms of positive rates. `gate_logits`: logits of the step sizes and decays.
All inputs are finite; a program needn't handle non-finite values.
Results may differ from a plain program's by a relative error of at most 0.0049.
Values may be sent and summed in bfloat16 or wider, within the bound.
A program may use at most 128 MiB of HBM per device.

v0:
```python
import jax
import jax.numpy as jnp
from jax import lax
from jax.sharding import PartitionSpec as P

KEY_HEAD_COUNT = 16
HV = 32
DK = 128
DV = 128
CONV = 4
SPAN = 64


TOP_PRECISION = lax.Precision.HIGHEST


def passed_along(array, axis, by):
    length = lax.axis_size(axis)
    pairs = [(i, i + by) for i in range(length) if 0 <= i + by < length]
    return lax.ppermute(array, axis, pairs)


def entering(value, axis, join, neutral):
    count, mine = (lax.axis_size(axis), lax.axis_index(axis))
    pieces = jax.tree.map(lambda part: lax.all_gather(part, axis), value)
    running = jax.tree.map(
        lambda part, zero: jnp.full_like(part, 0) + jnp.asarray(zero, part.dtype), value, neutral
    )

    def hop(position, running):
        longer = join(running, jax.tree.map(lambda part: part[position], pieces))
        return jax.tree.map(lambda new, old: jnp.where(position < mine, new, old), longer, running)

    return lax.fori_loop(0, count - 1, hop, running)


def l2_normed(inputs):
    return inputs * lax.rsqrt(jnp.sum(inputs * inputs, axis=-1, keepdims=True) + 1e-06)


def head_inputs(activated, logit_values, decay_log, step_bias):
    token_count = activated.shape[0]
    key_heads = activated.shape[1]
    head_group_ratio = logit_values.shape[-1]
    queries = jnp.repeat(l2_normed(activated[:, :, :DK]), head_group_ratio, axis=1)
    keys = jnp.repeat(l2_normed(activated[:, :, DK : 2 * DK]), head_group_ratio, axis=1)
    values = activated[:, :, 2 * DK :].reshape(token_count, key_heads * head_group_ratio, DV)
    step_size = jax.nn.sigmoid(
        logit_values[:, :, 0].reshape(token_count, key_heads * head_group_ratio)
    )
    decays = -jnp.exp(decay_log) * jax.nn.softplus(
        logit_values[:, :, 1].reshape(token_count, key_heads * head_group_ratio) + step_bias
    )
    return (queries, keys, values, step_size, decays)


def solve_block(matrix, target):
    return lax.linalg.triangular_solve(
        matrix, target, left_side=True, lower=True, unit_diagonal=True
    )


def span_terms(queries, keys, values, step_size, decays):
    block_len = queries.shape[0]
    cumulative = jnp.cumsum(decays, axis=0).T
    row_pos = lax.broadcasted_iota(jnp.int32, (block_len, block_len), 0)
    col_pos = lax.broadcasted_iota(jnp.int32, (block_len, block_len), 1)
    strict = row_pos > col_pos
    causal = row_pos >= col_pos
    log_gaps = cumulative[:, :, None] - cumulative[:, None, :]
    query_h = queries.transpose(1, 0, 2)
    key_h = keys.transpose(1, 0, 2)
    value_h = values.transpose(1, 0, 2)
    key_gram = jnp.einsum("htk,hsk->hts", key_h, key_h, precision=TOP_PRECISION)
    correlation = jnp.einsum("htk,hsk->hts", query_h, key_h, precision=TOP_PRECISION)
    step_h = step_size.T
    mixing = jnp.where(
        strict, step_h[:, :, None] * key_gram * jnp.exp(jnp.where(strict, log_gaps, 0.0)), 0.0
    )
    score_matrix = jnp.where(causal, correlation * jnp.exp(jnp.where(causal, log_gaps, 0.0)), 0.0)
    system = jnp.eye(block_len, dtype=jnp.float32) + mixing
    targets = jnp.concatenate(
        [step_h[:, :, None] * value_h, (step_h * jnp.exp(cumulative))[:, :, None] * key_h], axis=-1
    )
    solved = solve_block(system, targets)
    value_width = value_h.shape[-1]
    state_delta = solved[:, :, :value_width]
    key_vectors = solved[:, :, value_width:]
    final_key_row = jnp.exp(cumulative[:, -1:] - cumulative)[:, :, None] * key_h
    key_width = key_h.shape[-1]
    transition = jnp.exp(cumulative[:, -1])[:, None, None] * jnp.eye(
        key_width, dtype=jnp.float32
    ) - jnp.einsum("hsk,hsj->hkj", final_key_row, key_vectors, precision=TOP_PRECISION)
    state_increment = jnp.einsum(
        "qoz,qox->qzx", final_key_row, state_delta, precision=TOP_PRECISION
    )
    decayed_query = jnp.exp(cumulative)[:, :, None] * query_h
    return (score_matrix, state_delta, key_vectors, transition, state_increment, decayed_query)


def span_outputs(score_matrix, state_delta, key_vectors, decayed_query, state_list):
    state_projection = jnp.einsum("rbz,rzp->rbp", key_vectors, state_list, precision=TOP_PRECISION)
    return jnp.einsum(
        "rbz,rzp->rbp", decayed_query, state_list, precision=TOP_PRECISION
    ) + jnp.einsum(
        "icf,ifm->icm", score_matrix, state_delta - state_projection, precision=TOP_PRECISION
    )


def advance_state(transition, state_increment, state_list):
    return (
        jnp.einsum("hij,hjv->hiv", transition, state_list, precision=TOP_PRECISION)
        + state_increment
    )


def finish(core, gate_part, norm_gain):
    normed = core * lax.rsqrt(jnp.mean(core * core, axis=-1, keepdims=True) + 1e-06) * norm_gain
    return normed * jax.nn.silu(gate_part)


def compose_maps(earlier, later):
    product = jnp.einsum("hij,hjk->hik", later[0], earlier[0], precision=TOP_PRECISION)
    return (product, advance_state(later[0], later[1], earlier[1]))


def body(projected, gate_logits, conv_weight, decay_log, step_bias, norm_gain):
    head_group_ratio = HV // KEY_HEAD_COUNT
    channels = 2 * DK + head_group_ratio * DV
    features = channels + head_group_ratio * DV
    arrived, logits_in = (
        lax.all_to_all(projected, "head", split_axis=1, concat_axis=0, tiled=True),
        lax.all_to_all(gate_logits, "head", split_axis=1, concat_axis=0, tiled=True),
    )
    local_keys = arrived.shape[1] // features
    arrived = arrived.reshape(arrived.shape[0], local_keys, features)
    conv_in = arrived[:, :, :channels]
    gate_part = arrived[:, :, channels:].reshape(
        arrived.shape[0], local_keys * head_group_ratio, DV
    )
    seq_len = conv_in.shape[0]
    edge_rows = passed_along(conv_in[seq_len - CONV + 1 :], "ctx", 1)
    window = jnp.concatenate([edge_rows, conv_in], axis=0).astype(jnp.float32)
    conv_taps = conv_weight.astype(jnp.float32).reshape(CONV, local_keys, channels)
    mixed = conv_taps[0] * window[0:seq_len]
    for lag_step in range(1, CONV):
        mixed = mixed + conv_taps[lag_step] * window[lag_step : lag_step + seq_len]
    activated = jax.nn.silu(mixed)
    logit_values = logits_in.astype(jnp.float32).reshape(seq_len, local_keys, 2, head_group_ratio)
    queries, keys, values, step_size, decays = head_inputs(
        activated, logit_values, decay_log, step_bias
    )
    local_heads = queries.shape[1]
    blocks = seq_len // SPAN

    def blocked(array):
        return array.reshape((blocks, SPAN) + array.shape[1:])

    score_matrix, state_delta, key_vectors, transition, state_increment, decayed_query = jax.vmap(
        span_terms
    )(blocked(queries), blocked(keys), blocked(values), blocked(step_size), blocked(decays))
    identity = jnp.broadcast_to(jnp.eye(DK, dtype=jnp.float32), (local_heads, DK, DK))
    zero_state = jnp.zeros((local_heads, DK, DV), jnp.float32)

    def compose_only(carry, item):
        return (compose_maps(carry, item), None)

    (device_trans, device_add), unused = lax.scan(
        compose_only, (identity, zero_state), (transition, state_increment)
    )
    prefix = entering((device_trans, device_add), "ctx", compose_maps, (identity, zero_state))
    incoming = prefix[1]

    def replay(state_list, item):
        return (
            advance_state(item[3], item[4], state_list),
            span_outputs(item[0], item[1], item[2], item[5], state_list),
        )

    final_state, core_blocks = lax.scan(
        replay,
        incoming,
        (score_matrix, state_delta, key_vectors, transition, state_increment, decayed_query),
    )
    core = core_blocks.transpose(0, 2, 1, 3).reshape(seq_len, local_heads, DV)
    core_half = core.astype(jnp.bfloat16)
    core_back = lax.optimization_barrier(core_half).astype(jnp.float32)
    gated = (
        finish(core_back, gate_part.astype(jnp.float32), norm_gain)
        .astype(jnp.bfloat16)
        .reshape(seq_len, local_heads * DV)
    )
    result = lax.all_to_all(gated, "head", split_axis=0, concat_axis=1, tiled=True)
    return result


def solution(mesh):
    return jax.shard_map(
        body,
        mesh=mesh,
        in_specs=(
            P(("ctx", "head"), None),
            P(("ctx", "head"), None),
            P(None, "head"),
            P("head"),
            P("head"),
            P(),
        ),
        out_specs=P(("ctx", "head"), None),
        check_vma=False,
    )
```

profile of v0, /device:TPU:1, one launch (start us, length us, event | category | flops | bytes accessed | tf_op | source)
XLA Modules:
  0.0 550.8 jit_solution(3681274219364636020)
XLA Ops:
  8.0 10.1 %all-to-all-start = ((bf16[8,2,128]{2,1,0:T(2,128)(2,1)}), bf16[8,2,128]{2,1,0:T(2,128)(2,1)S(1)}, u32[]{:S(2)}, u32[]{:S(2)}) async-start(bf16[8,2,128]{2,1,0:T(2,128)(2,1)} %reshape.136), calls=%async_computation | async-start | bytes 8192 | tf_op jit(solution)/shard_map/all_to_all | solution.py:133
  19.6 2.1 copy.159
  22.6 4.1 all-to-all-start.1
  28.4 10.5 %all-to-all-done.1 = bf16[32,8,1536]{2,0,1:T(8,128)(2,1)S(1)} async-done(((bf16[32,8,1536]{2,0,1:T(8,128)(2,1)}), bf16[32,8,1536]{2,0,1:T(8,128)(2,1)S(1)}, u32[]{:S(2)}, u32[]{:S(2)}) %all-to-all-start.1) | async-done | bytes 786464 | tf_op jit(solution)/shard_map/all_to_all | solution.py:132
  41.8 1.9 divide_multiply_fusion
  47.9 78.6 %custom-call.3 = f32[4,4,1,64,64]{3,4,2,1,0:T(8,128)S(1)} custom-call(f32[4,4,1,64,64]{4,3,2,1,0:T(8,128)S(1)} %fusion.40), custom_call_target="InvertDiagBlocksLowerTriangular" | custom-call | tf_op jit(solution)/shard_map/vmap()/triangular_solve | solution.py:58
  127.6 2.0 fusion.58
  129.6 2.0 convolution_subtract_fusion.1
  131.7 3.5 while.40
  140.4 2.3 fusion.76
  142.7 1.8 fusion.34
  144.4 134.6 %all-gather.5.cloned.1.call-done = f32[256,128,128]{2,1,0:T(8,128)} async-done(((f32[4,128,128]{2,1,0:T(8,128)}), f32[256,128,128]{2,1,0:T(8,128)}) %all-gather.5.cloned.1.call-update) | async-done | bytes 16777232 | tf_op jit(solution)/shard_map/all_gather | solution.py:25
  279.1 140.9 %all-gather.7.cloned.1.call-done = f32[256,128,128]{2,1,0:T(8,128)} async-done(((f32[4,128,128]{2,1,0:T(8,128)}), f32[256,128,128]{2,1,0:T(8,128)}) %all-gather.7.cloned.1.call-update) | async-done | bytes 16777232 | tf_op jit(solution)/shard_map/all_gather | solution.py:25
  419.9 93.3 %while.41 = (s32[]{:T(128)}, f32[4,128,128]{2,1,0:T(8,128)S(1)}, s32[]{:T(128)}, f32[64,4,128,128]{3,2,1,0:T(8,128)}, f32[64,4,128,128]{3,2,1,0:T(8,128)}, /*index=5*/s32[]{:T(128)}, s32[]{:T(128)}) while((s32[]{:T(128)}, f32[4,128,128]{2,1,0:T(8,128)S(1)}, s32[]{:T(128)}, f32[64,4,128,128]{3,2,1,0:T(8,128)}, ...), condition=%wide.region_5.6_spmd.clone, body=%wide.region_4.5_spmd.clone.sunk | while | flops 100925440 | bytes 1837671 | solution.py:34
  437.8 1.4 fusion.117
  439.2 1.4 fusion.117
  440.7 1.4 fusion.117
  442.2 1.4 fusion.117
  443.7 1.4 fusion.117
  445.2 1.4 fusion.117
  448.1 1.4 fusion.117
  449.6 1.4 fusion.117
  451.1 1.4 fusion.117
  454.1 1.4 fusion.117
  455.5 1.4 fusion.117
  457.0 1.4 fusion.117
  458.5 1.4 fusion.117
  460.0 1.4 fusion.117
  461.5 1.4 fusion.117
  463.0 1.4 fusion.117
  513.3 15.9 %while.39 = (s32[]{:T(128)}, f32[4,128,128]{2,1,0:T(8,128)S(1)}, bf16[4,4,64,128]{3,2,0,1:T(8,128)(2,1)}, f32[4,4,128,128]{3,2,1,0:T(8,128)S(1)}, f32[4,4,128,12...) while((s32[]{:T(128)}, f32[4,128,128]{2,1,0:T(8,128)S(1)}, ...), condition=%wide.region_8.9_spmd, body=%wide.region_7.8_spmd.sunk | while | flops 226623488 | bytes 3279985 | solution.py:180
  531.9 11.4 %all_to_all.48 = bf16[8,32,512]{2,1,0:T(8,128)(2,1)S(1)} all-to-all(bf16[8,32,512]{2,1,0:T(8,128)(2,1)S(1)} %all_to_all.41), channel_id=1, replica_groups=mesh['ctx'=64,'head'=8] {'head'}, dimensions={0} | all-to-all | bytes 524288 | tf_op jit(solution)/shard_map/all_to_all | solution.py:193
  (226 shorter events, 109.1 us)
Async XLA Ops:
  8.0 14.6 %all-to-all-start = ((bf16[8,2,128]{2,1,0:T(2,128)(2,1)}), bf16[8,2,128]{2,1,0:T(2,128)(2,1)S(1)}, u32[]{:S(2)}, u32[]{:S(2)}) async-start(bf16[8,2,128]{2,1,0:T(2,128)(2,1)} %reshape.136), calls=%async_computation | async-start | bytes 8192 | tf_op jit(solution)/shard_map/all_to_all | solution.py:133
  22.6 16.3 %all-to-all-start.1 = ((bf16[32,8,1536]{2,0,1:T(8,128)(2,1)}), bf16[32,8,1536]{2,0,1:T(8,128)(2,1)S(1)}, u32[]{:S(2)}, u32[]{:S(2)}) async-start(bf16[32,8,1536]{2,0,1:T(8,128)(2,1)} %bitcast.96), calls=%async_computation.1 | async-start | bytes 1572864 | tf_op jit(solution)/shard_map/all_to_all | solution.py:132
  26.8 252.3 %all-gather.5.cloned.1.call-start = ((), (), s32[]{:S(2)}) async-start(), calls=%async_computation.3 | async-start | bytes 17039360 | tf_op jit(solution)/shard_map/all_gather | solution.py:25
  39.1 2.1 copy-start.3
  39.2 2.1 collective-permute-start
  127.6 2.0 copy-start.2
  135.2 0.7 copy-start
  135.2 0.9 copy-start.1
  135.2 395.2 %copy-start.5 = (f32[128]{0:T(128)S(1)}, f32[128]{0:T(128)}, u32[]{:S(2)}) copy-start(f32[128]{0:T(128)} %param.17) | copy-start | bytes 1540
  135.9 284.0 %all-gather.7.cloned.1.call-start = ((), (), s32[]{:S(2)}) async-start(), calls=%async_computation.4 | async-start | bytes 17039360 | tf_op jit(solution)/shard_map/all_gather | solution.py:25
  513.3 17.1 %copy-start.4 = (f32[256,4,128]{2,1,0:T(4,128)S(1)}, f32[256,4,128]{2,1,0:T(4,128)}, u32[]{:S(2)}) copy-start(f32[256,4,128]{2,1,0:T(4,128)} %reshape.110) | copy-start | bytes 1572868
Sparse Core Ops, SparseCore 0:
  136.0 142.9 all-gather.4
  282.1 137.8 all-gather.6
where the time goes:
time: 553 us; the launch traced here: 551 us
  waiting for transfers between devices  288 us (52%)
  matrix products  116 us (21%)
  other arithmetic  89.7 us (16%)
  starting transfers between devices  15.7 us (3%)
  between operations  13.8 us (2%)
  local copies, waits for them, and re-layouts  13.4 us (2%)
  blocking collectives  11.4 us (2%)
    all_gather x2, waiting for transfers between devices, entering(): pieces = jax.tree.map(lambda part: lax.all_gather(part, axis), value)  276 us
    dot_general x71, matrix products, advance_state(): jnp.einsum('hij,hjv->hiv', transition, state_list, precision=TOP_PRECISION)  92.8 us
    another operation x2, other arithmetic, solve_block(): lax.linalg.triangular_solve(matrix, target, left_side=True, lower=True, u...  78.6 us
    all_to_all x1, blocking collectives, body(): lax.all_to_all(gated, 'head', split_axis=0, concat_axis=1, tiled=True)  11.4 us
  transfers between devices with their start and end apart: 5, of which 5 were waited for; matrix products, arithmetic and copies ran while one was open for 2% of the time, Pallas kernels for 0%

commit v1 on v0

v1 whole, which is shorter than its diff:
```python
import jax
import jax.numpy as jnp
from jax import lax
from jax.sharding import PartitionSpec as P

KEY_HEAD_COUNT = 16
HV = 32
DK = 128
DV = 128
CONV = 4
SPAN = 64


TOP_PRECISION = lax.Precision.HIGHEST
ROW = 8


def passed_along(array, axis, by):
    length = lax.axis_size(axis)
    pairs = [(i, i + by) for i in range(length) if 0 <= i + by < length]
    return lax.ppermute(array, axis, pairs)


def l2_normed(inputs):
    return inputs * lax.rsqrt(jnp.sum(inputs * inputs, axis=-1, keepdims=True) + 1e-06)


def head_inputs(activated, logit_values, decay_log, step_bias):
    token_count = activated.shape[0]
    key_heads = activated.shape[1]
    head_group_ratio = logit_values.shape[-1]
    queries = jnp.repeat(l2_normed(activated[:, :, :DK]), head_group_ratio, axis=1)
    keys = jnp.repeat(l2_normed(activated[:, :, DK : 2 * DK]), head_group_ratio, axis=1)
    values = activated[:, :, 2 * DK :].reshape(token_count, key_heads * head_group_ratio, DV)
    step_size = jax.nn.sigmoid(
        logit_values[:, :, 0].reshape(token_count, key_heads * head_group_ratio)
    )
    decays = -jnp.exp(decay_log) * jax.nn.softplus(
        logit_values[:, :, 1].reshape(token_count, key_heads * head_group_ratio) + step_bias
    )
    return (queries, keys, values, step_size, decays)


def mm(spec, a, b):
    return jnp.einsum(spec, a, b, precision=TOP_PRECISION)


def unit_inverse(lower):
    n = lower.shape[-1]
    row = lax.broadcasted_iota(jnp.int32, (n, n), 0)
    col = lax.broadcasted_iota(jnp.int32, (n, n), 1)

    def joint(size):
        return (row // (2 * size) == col // (2 * size)) & (row // size != col // size)

    inverse = jnp.eye(n, dtype=jnp.float32) - jnp.where(joint(1), lower, 0.0)
    size = 2
    while size < n:
        cross = jnp.where(joint(size), lower, 0.0)
        inverse = inverse - mm("bij,bjk->bik", inverse, mm("bij,bjk->bik", cross, inverse))
        size *= 2
    return inverse


def span_terms(queries, keys, values, step_size, decays):
    n = queries.shape[1]
    cumulative = jnp.cumsum(decays, axis=1)
    row = lax.broadcasted_iota(jnp.int32, (n, n), 0)
    col = lax.broadcasted_iota(jnp.int32, (n, n), 1)
    gaps = jnp.exp(jnp.where(row >= col, cumulative[:, :, None] - cumulative[:, None, :], 0.0))
    both = mm("btk,bsk->bts", jnp.concatenate([keys, queries], axis=1), keys)
    mixing = jnp.where(row > col, step_size[:, :, None] * both[:, :n] * gaps, 0.0)
    score = jnp.where(row >= col, both[:, n:] * gaps, 0.0)
    grown = jnp.exp(cumulative)[:, :, None]
    step = step_size[:, :, None]
    targets = jnp.concatenate([step * grown * keys, -step * values], axis=-1)
    solved = mm("bij,bjk->bik", unit_inverse(mixing), targets)
    last = jnp.exp(cumulative[:, -1:] - cumulative)[:, :, None] * keys
    eye = (
        lax.broadcasted_iota(jnp.int32, (2 * DK, DK), 0)
        == lax.broadcasted_iota(jnp.int32, (2 * DK, DK), 1)
    ).astype(jnp.float32)
    step_map = jnp.exp(cumulative[:, -1])[:, None, None] * eye - mm("bsj,bsk->bjk", solved, last)
    reads = -mm("bts,bsj->btj", score, solved)
    return step_map, reads[:, :, :DK] + grown * queries, reads[:, :, DK:]


def compose(earlier, later):
    product = mm("...ij,...jk->...ik", earlier, later[..., :DK, :])
    return product + jnp.concatenate(
        [jnp.zeros_like(later[..., :DK, :]), later[..., DK:, :]], axis=-2
    )


def entering(total):
    heads = total.shape[0]
    count = lax.axis_size("ctx")
    rows = count // ROW
    parts = ROW // heads
    width = DV // parts
    along = [[r * ROW + z for z in range(ROW)] for r in range(rows)]
    across = [[r * ROW + z for r in range(rows)] for z in range(ROW)]
    mine = lax.axis_index("ctx") // ROW
    pieces = jnp.concatenate(
        [
            jnp.broadcast_to(total[None, :, :DK], (parts, heads, DK, DK)),
            total[:, DK:].reshape(heads, parts, width, DK).transpose(1, 0, 2, 3),
        ],
        axis=2,
    ).reshape(ROW, DK + width, DK)
    got = lax.all_to_all(pieces, "ctx", 0, 0, axis_index_groups=along, tiled=True)
    eye = (
        lax.broadcasted_iota(jnp.int32, (DK + width, DK), 0)
        == lax.broadcasted_iota(jnp.int32, (DK + width, DK), 1)
    ).astype(jnp.float32)
    prefixes = [eye, got[0]]
    for z in range(1, ROW):
        prefixes.append(compose(prefixes[-1], got[z]))
    sent = jnp.broadcast_to(prefixes[-1][None], (rows,) + prefixes[-1].shape)
    row_maps = lax.all_to_all(sent, "ctx", 0, 0, axis_index_groups=across, tiled=True)
    state = jnp.where(mine > 0, row_maps[0, DK:], 0.0)
    for r in range(1, rows - 1):
        longer = mm("ij,jk->ik", state, row_maps[r, :DK]) + row_maps[r, DK:]
        state = jnp.where(r < mine, longer, state)
    stack = jnp.stack(prefixes[:ROW])
    states = mm("vj,zjk->zvk", state, stack[:, :DK]) + stack[:, DK:]
    back = lax.all_to_all(states, "ctx", 0, 0, axis_index_groups=along, tiled=True)
    return back.reshape(parts, heads, width, DK).transpose(1, 0, 2, 3).reshape(heads, DV, DK)


def finish(core, gate_part, norm_gain):
    normed = core * lax.rsqrt(jnp.mean(core * core, axis=-1, keepdims=True) + 1e-06) * norm_gain
    return normed * jax.nn.silu(gate_part)


def body(projected, gate_logits, conv_weight, decay_log, step_bias, norm_gain):
    head_group_ratio = HV // KEY_HEAD_COUNT
    channels = 2 * DK + head_group_ratio * DV
    features = channels + head_group_ratio * DV
    arrived, logits_in = (
        lax.all_to_all(projected, "head", split_axis=1, concat_axis=0, tiled=True),
        lax.all_to_all(gate_logits, "head", split_axis=1, concat_axis=0, tiled=True),
    )
    local_keys = arrived.shape[1] // features
    arrived = arrived.reshape(arrived.shape[0], local_keys, features)
    conv_in = arrived[:, :, :channels]
    gate_part = arrived[:, :, channels:].reshape(
        arrived.shape[0], local_keys * head_group_ratio, DV
    )
    seq_len = conv_in.shape[0]
    edge_rows = passed_along(conv_in[seq_len - CONV + 1 :], "ctx", 1)
    window = jnp.concatenate([edge_rows, conv_in], axis=0).astype(jnp.float32)
    conv_taps = conv_weight.astype(jnp.float32).reshape(CONV, local_keys, channels)
    mixed = conv_taps[0] * window[0:seq_len]
    for lag_step in range(1, CONV):
        mixed = mixed + conv_taps[lag_step] * window[lag_step : lag_step + seq_len]
    activated = jax.nn.silu(mixed)
    logit_values = logits_in.astype(jnp.float32).reshape(seq_len, local_keys, 2, head_group_ratio)
    queries, keys, values, step_size, decays = head_inputs(
        activated, logit_values, decay_log, step_bias
    )
    local_heads = queries.shape[1]
    blocks = seq_len // SPAN

    def blocked(array):
        array = array.reshape((blocks, SPAN) + array.shape[1:])
        return jnp.moveaxis(array, 2, 1).reshape((blocks * local_heads, SPAN) + array.shape[3:])

    step_map, reads, adds = span_terms(
        blocked(queries), blocked(keys), blocked(values), blocked(step_size), blocked(decays)
    )
    step_map = step_map.reshape(blocks, local_heads, 2 * DK, DK)
    reads = reads.reshape(blocks, local_heads, SPAN, DK)
    adds = adds.reshape(blocks, local_heads, SPAN, DV)
    maps = [step_map[0]]
    for b in range(1, blocks):
        maps.append(compose(maps[-1], step_map[b]))
    state = entering(maps[-1])
    later = mm("bhtk,bhjk->bhtj", reads[1:], jnp.stack(maps[:-1]))
    reads = jnp.concatenate([reads[:1], later[..., :DK]])
    adds = jnp.concatenate([adds[:1], adds[1:] + later[..., DK:]])
    core = mm("bhtk,hvk->bhtv", reads, state) + adds
    core = core.transpose(0, 2, 1, 3).reshape(seq_len, local_heads, DV)
    core_half = core.astype(jnp.bfloat16)
    core_back = lax.optimization_barrier(core_half).astype(jnp.float32)
    gated = (
        finish(core_back, gate_part.astype(jnp.float32), norm_gain)
        .astype(jnp.bfloat16)
        .reshape(seq_len, local_heads * DV)
    )
    result = lax.all_to_all(gated, "head", split_axis=0, concat_axis=1, tiled=True)
    return result


def solution(mesh):
    return jax.shard_map(
        body,
        mesh=mesh,
        in_specs=(
            P(("ctx", "head"), None),
            P(("ctx", "head"), None),
            P(None, "head"),
            P("head"),
            P("head"),
            P(),
        ),
        out_specs=P(("ctx", "head"), None),
        check_vma=False,
    )
```

time: 553 us -> 177 us (0.32)
  waiting for transfers between devices: 288 us -> 53.5 us
  other arithmetic: 89.7 us -> 10.8 us
  matrix products: 116 us -> 45.6 us
  starting transfers between devices: 15.7 us -> 36 us
  between operations: 13.8 us -> 0.69 us
    all_gather x2 -> x0, waiting for transfers between devices: 276 us -> none  [entering(): pieces = jax.tree.map(lambda part: lax.all_gather(part, axis), value)]
    another operation x3 -> x1, other arithmetic: 78.8 us -> 0.22 us  [span_terms(): cumulative = jnp.cumsum(decays, axis=1)]
    dot_general x91 -> x33, matrix products: 115 us -> 45.6 us  [mm(): return jnp.einsum(spec, a, b, precision=TOP_PRECISION)]
    all_to_all x0 -> x3, waiting for transfers between devices: none -> 41.3 us  [the longest x1 21 us: entering(): lax.all_to_all(pieces, 'ctx', 0, 0, axis_index_groups=along, tiled=True)]
    all_to_all x0 -> x3, starting transfers between devices: none -> 20.5 us  [the longest x1 9.26 us: entering(): lax.all_to_all(pieces, 'ctx', 0, 0, axis_index_groups=along, tiled=True)]
  transfers between devices with their start and end apart: 5 -> 6, of which waited for: 5 -> 6; matrix products, arithmetic and copies ran while one was open for 2% -> 9% of each run, Pallas kernels for 0% -> 0%
where the time goes in v1:
time: 177 us; the launch traced here: 176 us
  waiting for transfers between devices  53.5 us (30%)
  matrix products  45.6 us (26%)
  starting transfers between devices  36 us (20%)
  local copies, waits for them, and re-layouts  15 us (8%)
  blocking collectives  14.3 us (8%)
  other arithmetic  10.8 us (6%)
    dot_general x33, matrix products, mm(): return jnp.einsum(spec, a, b, precision=TOP_PRECISION)  45.6 us
    all_to_all x1, waiting for transfers between devices, entering(): lax.all_to_all(pieces, 'ctx', 0, 0, axis_index_groups=along, tiled=True)  21 us
    all_to_all x1, blocking collectives, body(): lax.all_to_all(gated, 'head', split_axis=0, concat_axis=1, tiled=True)  14.3 us
    all_to_all x1, waiting for transfers between devices, entering(): lax.all_to_all(sent, 'ctx', 0, 0, axis_index_groups=across, tiled=True)  12 us
    all_to_all x1, waiting for transfers between devices, body(): lax.all_to_all(projected, 'head', split_axis=1, concat_axis=0, tiled=True)  11.3 us
    all_to_all x1, starting transfers between devices, body(): lax.all_to_all(gate_logits, 'head', split_axis=1, concat_axis=0, tiled=True)  10.1 us
    all_to_all x1, starting transfers between devices, entering(): lax.all_to_all(pieces, 'ctx', 0, 0, axis_index_groups=along, tiled=True)  9.26 us
    all_to_all x1, waiting for transfers between devices, entering(): lax.all_to_all(states, 'ctx', 0, 0, axis_index_groups=along, tiled=True)  8.22 us
  transfers between devices with their start and end apart: 6, of which 6 were waited for; matrix products, arithmetic and copies ran while one was open for 9% of the time, Pallas kernels for 0%

profile of v1, /device:TPU:1, one launch (start us, length us, event | category | flops | bytes accessed | tf_op | source)
XLA Modules:
  0.0 175.9 jit_solution(14695787647732673961)
XLA Ops:
  1.5 10.1 %all-to-all-start = ((bf16[8,2,128]{2,1,0:T(2,128)(2,1)}), bf16[8,2,128]{2,1,0:T(2,128)(2,1)S(1)}, u32[]{:S(2)}, u32[]{:S(2)}) async-start(bf16[8,2,128]{2,1,0:T(2,128)(2,1)} %reshape.253), calls=%async_computation | async-start | bytes 8192 | tf_op jit(solution)/shard_map/all_to_all | solution.py:142
  13.4 2.1 %copy.115 = bf16[4,8,8,1536]{3,2,0,1:T(8,128)(2,1)} copy(bf16[4,8,8,1536]{3,2,1,0:T(8,128)(2,1)} %bitcast.241) | data formatting | bytes 1572864 | tf_op jit(solution)/shard_map/all_to_all | solution.py:141
  16.1 4.2 %all-to-all-start.1 = ((bf16[32,8,1536]{2,0,1:T(8,128)(2,1)}), bf16[32,8,1536]{2,0,1:T(8,128)(2,1)S(1)}, u32[]{:S(2)}, u32[]{:S(2)}) async-start(bf16[32,8,1536]{2,0,1:T(8,128)(2,1)} %bitcast.222), calls=%async_computation.1 | async-start | bytes 1572864 | tf_op jit(solution)/shard_map/all_to_all | solution.py:141
  21.2 11.3 %all-to-all-done.1 = bf16[32,8,1536]{2,0,1:T(8,128)(2,1)S(1)} async-done(((bf16[32,8,1536]{2,0,1:T(8,128)(2,1)}), bf16[32,8,1536]{2,0,1:T(8,128)(2,1)S(1)}, u32[]{:S(2)}, u32[]{:S(2)}) %all-to-all-start.1) | async-done | bytes 786464 | tf_op jit(solution)/shard_map/all_to_all | solution.py:141
  32.7 1.3 collective-permute-start
  35.3 1.9 %divide_multiply_fusion = f32[256,2,512]{2,1,0:T(2,128)S(1)} fusion(f32[259,2,512]{2,1,0:T(2,128)S(1)} %maximum_convert_fusion, f32[2,512]{1,0:T(2,128)S(1)} %mul.186, f32[2,512]{1,0:T(2,128)S(1)} %mul.183, f32[2,512]{1,0:T(2,128)S(1)} %mul.180, f32[2,512]{1,0:T(2,128)S(1)} %mul.177), kind=kLoop, calls=%fused_computation.42 | loop fusion | flops 2883584 | bytes 5259264 | tf_op jit(solution)/shard_map/jit(silu)/mul | solution.py:157
  40.0 2.1 %fusion.20 = f32[16,128,64]{1,2,0:T(8,128)S(1)} fusion(f32[16,64,128]{2,1,0:T(8,128)S(1)} %bitcast.223, f32[16,64,128]{2,1,0:T(8,128)S(1)} %bitcast.225), kind=kOutput, calls=%fused_computation.50 | convolution fusion | flops 201588736 | bytes 1572864 | tf_op jit(solution)/shard_map/btk,bsk->bts/dot_general | solution.py:45
  42.1 1.4 fusion.49
  44.7 1.2 fusion.47
  47.0 1.2 fusion.45
  49.2 1.2 fusion.43
  51.4 1.2 fusion.41
  55.2 4.1 %multiply_subtract_fusion = f32[16,256,128]{2,1,0:T(8,128)S(1)} fusion(f32[16,64,256]{2,1,0:T(8,128)S(1)} %fusion.24, f32[256,128]{1,0:T(8,128)S(1)} %fusion.74, f32[16]{0:T(128)S(1)} %exp.50, f32[16,64,128]{2,1,0:T(8,128)S(1)} %bitcast.224, f32[16,64]{1,0:T(8,128)S(1)} %get-tuple-element.30), kind=kOutput, calls=%fused_computation | convolution fusion | flops 403832832 | bytes 3805248 | tf_op jit(solution)/shard_map/bsj,bsk->bjk/dot_general | solution.py:45
  62.3 9.3 %all-to-all-start.2 = ((f32[8,192,128]{2,1,0:T(8,128)}), f32[8,192,128]{2,1,0:T(8,128)}, u32[]{:S(2)}, u32[]{:S(2)}) async-start(f32[8,192,128]{2,1,0:T(8,128)} %bitcast.228), calls=%async_computation.2 | async-start | bytes 1572864 | tf_op jit(solution)/shard_map/all_to_all | solution.py:111
  72.3 21.0 %all-to-all-done.2 = f32[8,192,128]{2,1,0:T(8,128)} async-done(((f32[8,192,128]{2,1,0:T(8,128)}), f32[8,192,128]{2,1,0:T(8,128)}, u32[]{:S(2)}, u32[]{:S(2)}) %all-to-all-start.2) | async-done | bytes 786464 | tf_op jit(solution)/shard_map/all_to_all | solution.py:111
  94.2 1.5 slice_dynamic-update-slice_fusion
  95.7 1.8 %bitcast_dynamic-update-slice_fusion.5 = (f32[8,192,128]{2,1,0:T(8,128)}, f32[192,128]{1,0:T(8,128)S(1)}) fusion(f32[8,192,128]{2,1,0:T(8,128)} %slice_dynamic-update-slice_fusion, f32[64,128]{1,0:T(8,128)S(1)} %get-tuple-element.24, f32[8,192,128]{2,1,0:T(8,128)} %all-to-all-done.2), kind=kOutput, calls=%fused_computation.133 | convolution fusion | flops 37773312 | bytes 393216 | tf_op jit(solution)/shard_map/...ij,...jk->...ik/dot_general | solution.py:45
  97.5 1.7 bitcast_dynamic-update-slice_fusion.4
  99.2 1.7 bitcast_dynamic-update-slice_fusion.3
  100.9 1.7 bitcast_dynamic-update-slice_fusion.2
  102.6 1.7 bitcast_dynamic-update-slice_fusion.1
  104.3 1.7 bitcast_dynamic-update-slice_fusion
  108.1 7.8 %all-to-all-start.3 = ((f32[8,192,128]{2,1,0:T(8,128)}), f32[8,192,128]{2,1,0:T(8,128)}, u32[]{:S(2)}, u32[]{:S(2)}) async-start(f32[8,192,128]{2,1,0:T(8,128)} %broadcast_in_dim.87), calls=%async_computation.3 | async-start | bytes 1572864 | tf_op jit(solution)/shard_map/all_to_all | solution.py:120
  115.9 1.9 %slice_convert_fusion = f32[256,2,256]{2,1,0:T(2,128)} fusion(bf16[256,2,768]{2,1,0:T(2,128)(2,1)} %copy-done.6), kind=kLoop, calls=%fused_computation.93 | loop fusion | flops 131072 | bytes 786432 | tf_op jit(solution)/shard_map/convert_element_type | solution.py:187
  117.8 2.3 %reshape.227 = f32[256,4,128]{2,1,0:T(4,128)} reshape(f32[256,2,256]{2,1,0:T(2,128)} %slice_convert_fusion) | data formatting | bytes 1048576 | tf_op jit(solution)/shard_map/convert_element_type | solution.py:187
  120.2 2.6 %convolution_negate_fusion = f32[16,64,256]{2,1,0:T(8,128)S(1)} fusion(f32[16,64,256]{2,1,0:T(8,128)} %copy-done, f32[16,128,64]{1,2,0:T(8,128)S(1)} %fusion.20, f32[16,64]{1,0:T(8,128)S(1)} %reduce_window_sum.11, pred[64,64]{0,1:T(8,128)(4,1)S(1)} %get-tuple-element.71), kind=kOutput, calls=%fused_computation.7 | convolution fusion | flops 201850880 | bytes 2646016 | tf_op jit(solution)/shard_map/bts,bsj->btj/dot_general | solution.py:45
  124.4 1.8 %fusion = f32[3,4,64,256]{3,2,1,0:T(8,128)S(1)} fusion(f32[3,4,64,128]{3,2,1,0:T(8,128)S(1)} %bitcast.236, f32[1,4,256,128]{3,2,1,0:T(8,128)S(1)} %bitcast.227, f32[1,4,256,128]{3,2,1,0:T(8,128)S(1)} %bitcast.226, f32[1,4,256,128]{3,2,1,0:T(8,128)S(1)} %slice_bitcast_fusion), kind=kOutput, calls=%fused_computation.1 | convolution fusion | flops 302776320 | bytes 2752512 | tf_op jit(solution)/shard_map/bhtk,bhjk->bhtj/dot_general | solution.py:45
  126.2 12.0 %all-to-all-done.3 = f32[8,192,128]{2,1,0:T(8,128)} async-done(((f32[8,192,128]{2,1,0:T(8,128)}), f32[8,192,128]{2,1,0:T(8,128)}, u32[]{:S(2)}, u32[]{:S(2)}) %all-to-all-start.3) | async-done | bytes 786464 | tf_op jit(solution)/shard_map/all_to_all | solution.py:120
  144.5 2.2 %fusion.8 = f32[8,64,128]{2,1,0:T(8,128)} fusion(f32[64,128,1]{1,0,2:T(8,128)S(1)} %fusion.11, f32[8,192,128]{2,1,0:T(8,128)} %get-tuple-element.49), kind=kOutput, calls=%fused_computation.20 | convolution fusion | flops 100728832 | bytes 1081344 | tf_op jit(solution)/shard_map/vj,zjk->zvk/dot_general | solution.py:45
  146.7 3.4 %all-to-all-start.4 = ((f32[8,64,128]{2,1,0:T(8,128)}), f32[8,64,128]{2,1,0:T(8,128)S(1)}, u32[]{:S(2)}, u32[]{:S(2)}) async-start(f32[8,64,128]{2,1,0:T(8,128)} %fusion.8), calls=%async_computation.4 | async-start | bytes 524288 | tf_op jit(solution)/shard_map/all_to_all | solution.py:127
  151.2 8.2 %all-to-all-done.4 = f32[8,64,128]{2,1,0:T(8,128)S(1)} async-done(((f32[8,64,128]{2,1,0:T(8,128)}), f32[8,64,128]{2,1,0:T(8,128)S(1)}, u32[]{:S(2)}, u32[]{:S(2)}) %all-to-all-start.4) | async-done | bytes 262176 | tf_op jit(solution)/shard_map/all_to_all | solution.py:127
  160.9 14.3 %all_to_all.63 = bf16[8,32,512]{2,1,0:T(8,128)(2,1)S(1)} all-to-all(bf16[8,32,512]{2,1,0:T(8,128)(2,1)S(1)} %all_to_all.53), channel_id=1, replica_groups=mesh['ctx'=64,'head'=8] {'head'}, dimensions={0} | all-to-all | bytes 524288 | tf_op jit(solution)/shard_map/all_to_all | solution.py:191
  (118 shorter events, 33.1 us)
Async XLA Ops:
  0.0 20.7 %copy-start.10 = (f32[4]{0:T(128)S(1)}, f32[4]{0:T(128)}, u32[]{:S(2)}) copy-start(f32[4]{0:T(128)} %param.10) | copy-start | bytes 52
  1.5 14.6 %all-to-all-start = ((bf16[8,2,128]{2,1,0:T(2,128)(2,1)}), bf16[8,2,128]{2,1,0:T(2,128)(2,1)S(1)}, u32[]{:S(2)}, u32[]{:S(2)}) async-start(bf16[8,2,128]{2,1,0:T(2,128)(2,1)} %reshape.253), calls=%async_computation | async-start | bytes 8192 | tf_op jit(solution)/shard_map/all_to_all | solution.py:142
  16.1 16.4 %all-to-all-start.1 = ((bf16[32,8,1536]{2,0,1:T(8,128)(2,1)}), bf16[32,8,1536]{2,0,1:T(8,128)(2,1)S(1)}, u32[]{:S(2)}, u32[]{:S(2)}) async-start(bf16[32,8,1536]{2,0,1:T(8,128)(2,1)} %bitcast.222), calls=%async_computation.1 | async-start | bytes 1572864 | tf_op jit(solution)/shard_map/all_to_all | solution.py:141
  32.7 2.1 %copy-start.6 = (bf16[256,2,768]{2,1,0:T(2,128)(2,1)}, bf16[256,2,768]{2,1,0:T(2,128)(2,1)S(1)}, u32[]{:S(2)}) copy-start(bf16[256,2,768]{2,1,0:T(2,128)(2,1)S(1)} %reshape.218) | copy-start | bytes 2359300
  32.7 2.1 %collective-permute-start = (bf16[3,2,512]{2,1,0:T(2,128)(2,1)S(1)}, bf16[3,2,512]{2,1,0:T(2,128)(2,1)S(1)}, u32[]{:S(2)}, u32[]{:S(2)}) collective-permute-start(bf16[3,2,512]{2,1,0:T(2,128)(2,1)S(1)} %slice.382), channel_id=1, source_target_pairs={{0,8},{8,16},{16,24},{24,32},{32,40},{40,48},{48,56},{56,64},{64,7... | collective-permute-start | bytes 18440 | tf_op jit(solution)/shard_map/ppermute | solution.py:21
  55.1 4.2 %copy-start = (f32[16,64,256]{2,1,0:T(8,128)}, f32[16,64,256]{2,1,0:T(8,128)S(1)}, u32[]{:S(2)}) copy-start(f32[16,64,256]{2,1,0:T(8,128)S(1)} %fusion.24) | copy-start | bytes 3145732
  59.9 1.3 copy-start.1
  60.6 0.8 copy-start.3
  62.3 31.0 %all-to-all-start.2 = ((f32[8,192,128]{2,1,0:T(8,128)}), f32[8,192,128]{2,1,0:T(8,128)}, u32[]{:S(2)}, u32[]{:S(2)}) async-start(f32[8,192,128]{2,1,0:T(8,128)} %bitcast.228), calls=%async_computation.2 | async-start | bytes 1572864 | tf_op jit(solution)/shard_map/all_to_all | solution.py:111
  108.1 30.1 %all-to-all-start.3 = ((f32[8,192,128]{2,1,0:T(8,128)}), f32[8,192,128]{2,1,0:T(8,128)}, u32[]{:S(2)}, u32[]{:S(2)}) async-start(f32[8,192,128]{2,1,0:T(8,128)} %broadcast_in_dim.87), calls=%async_computation.3 | async-start | bytes 1572864 | tf_op jit(solution)/shard_map/all_to_all | solution.py:120
  122.7 1.0 copy-start.5
  122.7 1.4 copy-start.2
  122.8 1.6 copy-start.4
  143.4 16.0 %copy-start.8 = (f32[1,4,64,128]{3,2,1,0:T(8,128)S(1)}, f32[1,4,64,128]{3,2,1,0:T(8,128)}, u32[]{:S(2)}) copy-start(f32[1,4,64,128]{3,2,1,0:T(8,128)} %slice_bitcast_fusion.2) | copy-start | bytes 393220
  146.7 12.7 %all-to-all-start.4 = ((f32[8,64,128]{2,1,0:T(8,128)}), f32[8,64,128]{2,1,0:T(8,128)S(1)}, u32[]{:S(2)}, u32[]{:S(2)}) async-start(f32[8,64,128]{2,1,0:T(8,128)} %fusion.8), calls=%async_computation.4 | async-start | bytes 524288 | tf_op jit(solution)/shard_map/all_to_all | solution.py:127
  151.0 9.2 %copy-start.7 = (f32[256,4,128]{2,1,0:T(4,128)S(1)}, f32[256,4,128]{2,1,0:T(4,128)}, u32[]{:S(2)}) copy-start(f32[256,4,128]{2,1,0:T(4,128)} %reshape.227) | copy-start | bytes 1572868
  151.1 9.2 %copy-start.9 = (f32[128]{0:T(128)S(1)}, f32[128]{0:T(128)}, u32[]{:S(2)}) copy-start(f32[128]{0:T(128)} %param.11) | copy-start | bytes 1540

commit v2 on v1

--- a/solution.py
+++ b/solution.py
@@ -1,6 +1,8 @@
 import jax
 import jax.numpy as jnp
 from jax import lax
+from jax.experimental import pallas as pl
+from jax.experimental.pallas import tpu as pltpu
 from jax.sharding import PartitionSpec as P
 
 KEY_HEAD_COUNT = 16
@@ -92,15 +94,132 @@
     )
 
 
-def entering(total):
+def nn(a, b):
+    return lax.dot_general(
+        a, b, (((1,), (0,)), ((), ())),
+        precision=TOP_PRECISION, preferred_element_type=jnp.float32,
+    )
+
+
+def nt(a, b):
+    return lax.dot_general(
+        a, b, (((1,), (1,)), ((), ())),
+        precision=TOP_PRECISION, preferred_element_type=jnp.float32,
+    )
+
+
+OFFSETS = (4, 3, 5, 2, 6, 1, 7)
+
+
+def carry_kernel(
+    pieces, maps, reads, adds, arrived, gain, out,
+    got, prefix, row_total, row_maps, states, entered, core_reads, core_adds,
+    send_a, recv_a, send_b, recv_b, send_c, recv_c,
+):
+    blocks, heads = reads.shape[:2]
+    count = ROW
+    mine = lax.axis_index("ctx")
+    r, z = mine // count, lax.rem(mine, count)
+
+    def in_row(k):
+        return r * count + lax.rem(z + k, count)
+
+    def in_column(k):
+        return lax.rem(r + k, count) * count + z
+
+    barrier = pltpu.get_barrier_semaphore()
+    for k in range(1, count):
+        for peer in (in_row(k), in_column(k)):
+            pl.semaphore_signal(
+                barrier, inc=1, device_id={"ctx": peer}, device_id_type=pl.DeviceIdType.MESH
+            )
+    pl.semaphore_wait(barrier, 2 * (count - 1))
+
+    def send(source, target, send_sem, recv_sem, peer):
+        copy = pltpu.make_async_remote_copy(
+            src_ref=source, dst_ref=target, send_sem=send_sem, recv_sem=recv_sem,
+            device_id={"ctx": peer}, device_id_type=pl.DeviceIdType.MESH,
+        )
+        copy.start()
+        return copy
+
+    first = [
+        send(
+            pieces.at[lax.rem(z + k, count)], got.at[z],
+            send_a.at[k], recv_a.at[k], in_row(k),
+        )
+        for k in OFFSETS
+    ]
+    got[z] = pieces[z]
+
+    def affine(i, carry):
+        b, h = i // heads, lax.rem(i, heads)
+        both = nt(reads[b + 1, h], maps[b, h])
+        at = pl.ds(pl.multiple_of((b + 1) * SPAN, SPAN), SPAN)
+        core_reads[h, at, :] = both[:, :DK]
+        core_adds[h, at, :] = both[:, DK:] + adds[b + 1, h]
+        return carry
+
+    lax.fori_loop(0, (blocks - 1) * heads, affine, 0)
+    for h in range(heads):
+        core_reads[h, :SPAN, :] = reads[0, h]
+        core_adds[h, :SPAN, :] = adds[0, h]
+
+    for copy in first:
+        copy.wait()
+    prefix[1] = got[0]
+
+    def advance(c, carry):
+        product = nn(prefix[c], got[c, :DK, :])
+        prefix[c + 1, :DK, :] = product[:DK]
+        prefix[c + 1, DK:, :] = product[DK:] + got[c, DK:, :]
+        return carry
+
+    lax.fori_loop(1, count - 1, advance, 0)
+    product = nn(prefix[count - 1], got[count - 1, :DK, :])
+    row_total[:DK, :] = product[:DK]
+    row_total[DK:, :] = product[DK:] + got[count - 1, DK:, :]
+    second = [
+        send(row_total, row_maps.at[r], send_b.at[k], recv_b.at[k], in_column(k))
+        for k in OFFSETS
+    ]
+    row_maps[r] = row_total[...]
+    for copy in second:
+        copy.wait()
+    state = jnp.where(r > 0, row_maps[0, DK:, :], 0.0)
+    for c in range(1, count - 1):
+        longer = nn(state, row_maps[c, :DK, :]) + row_maps[c, DK:, :]
+        state = jnp.where(c < r, longer, state)
+    states[0] = state
+    for c in range(1, count):
+        states[c] = nn(state, prefix[c, :DK, :]) + prefix[c, DK:, :]
+    third = [
+        send(
+            states.at[lax.rem(z + k, count)], entered.at[z],
+            send_c.at[k], recv_c.at[k], in_row(k),
+        )
+        for k in OFFSETS
+    ]
+    entered[z] = states[z]
+    for copy in third:
+        copy.wait()
+    features = arrived.shape[1] // heads
+    for h in range(heads):
+        entering = jnp.concatenate([entered[h + heads * p] for p in range(count // heads)], axis=0)
+        core = nt(core_reads[h], entering) + core_adds[h]
+        core = core.astype(jnp.bfloat16).astype(jnp.float32)
+        at = (h // 2) * 2 * features + 2 * DK + 2 * DV + (h % 2) * DV
+        gate = arrived[:, at : at + DV].astype(jnp.float32)
+        scale = lax.rsqrt(jnp.mean(core * core, axis=-1, keepdims=True) + 1e-06)
+        normed = core * scale * gain[...]
+        out[:, h * DV : (h + 1) * DV] = (normed * jax.nn.silu(gate)).astype(jnp.bfloat16)
+
+
+def carried(total, maps, reads, adds, arrived, gain):
     heads = total.shape[0]
-    count = lax.axis_size("ctx")
-    rows = count // ROW
     parts = ROW // heads
     width = DV // parts
-    along = [[r * ROW + z for z in range(ROW)] for r in range(rows)]
-    across = [[r * ROW + z for r in range(rows)] for z in range(ROW)]
-    mine = lax.axis_index("ctx") // ROW
+    seq_len = arrived.shape[0]
     pieces = jnp.concatenate(
         [
             jnp.broadcast_to(total[None, :, :DK], (parts, heads, DK, DK)),
@@ -108,29 +227,28 @@
         ],
         axis=2,
     ).reshape(ROW, DK + width, DK)
-    got = lax.all_to_all(pieces, "ctx", 0, 0, axis_index_groups=along, tiled=True)
-    eye = (
-        lax.broadcasted_iota(jnp.int32, (DK + width, DK), 0)
-        == lax.broadcasted_iota(jnp.int32, (DK + width, DK), 1)
-    ).astype(jnp.float32)
-    prefixes = [eye, got[0]]
-    for z in range(1, ROW):
-        prefixes.append(compose(prefixes[-1], got[z]))
-    sent = jnp.broadcast_to(prefixes[-1][None], (rows,) + prefixes[-1].shape)
-    row_maps = lax.all_to_all(sent, "ctx", 0, 0, axis_index_groups=across, tiled=True)
-    state = jnp.where(mine > 0, row_maps[0, DK:], 0.0)
-    for r in range(1, rows - 1):
-        longer = mm("ij,jk->ik", state, row_maps[r, :DK]) + row_maps[r, DK:]
-        state = jnp.where(r < mine, longer, state)
-    stack = jnp.stack(prefixes[:ROW])
-    states = mm("vj,zjk->zvk", state, stack[:, :DK]) + stack[:, DK:]
-    back = lax.all_to_all(states, "ctx", 0, 0, axis_index_groups=along, tiled=True)
-    return back.reshape(parts, heads, width, DK).transpose(1, 0, 2, 3).reshape(heads, DV, DK)
-
-
-def finish(core, gate_part, norm_gain):
-    normed = core * lax.rsqrt(jnp.mean(core * core, axis=-1, keepdims=True) + 1e-06) * norm_gain
-    return normed * jax.nn.silu(gate_part)
+    piece = (ROW, DK + width, DK)
+    half = (ROW, width, DK)
+    full = (heads, seq_len, DK)
+    vmem = pl.BlockSpec(memory_space=pltpu.VMEM)
+    return pl.pallas_call(
+        carry_kernel,
+        out_shape=jax.ShapeDtypeStruct((seq_len, heads * DV), jnp.bfloat16),
+        in_specs=[vmem] * 6,
+        out_specs=vmem,
+        scratch_shapes=[
+            pltpu.VMEM(piece, jnp.float32),
+            pltpu.VMEM(piece, jnp.float32),
+            pltpu.VMEM(piece[1:], jnp.float32),
+            pltpu.VMEM(piece, jnp.float32),
+            pltpu.VMEM(half, jnp.float32),
+            pltpu.VMEM(half, jnp.float32),
+            pltpu.VMEM(full, jnp.float32),
+            pltpu.VMEM(full, jnp.float32),
+        ]
+        + [pltpu.SemaphoreType.DMA((ROW,))] * 6,
+        compiler_params=pltpu.CompilerParams(collective_id=0, has_side_effects=True),
+    )(pieces, maps, reads, adds, arrived, gain)
 
 
 def body(projected, gate_logits, conv_weight, decay_log, step_bias, norm_gain):
@@ -142,11 +260,9 @@
         lax.all_to_all(gate_logits, "head", split_axis=1, concat_axis=0, tiled=True),
     )
     local_keys = arrived.shape[1] // features
+    flat = arrived
     arrived = arrived.reshape(arrived.shape[0], local_keys, features)
     conv_in = arrived[:, :, :channels]
-    gate_part = arrived[:, :, channels:].reshape(
-        arrived.shape[0], local_keys * head_group_ratio, DV
-    )
     seq_len = conv_in.shape[0]
     edge_rows = passed_along(conv_in[seq_len - CONV + 1 :], "ctx", 1)
     window = jnp.concatenate([edge_rows, conv_in], axis=0).astype(jnp.float32)
@@ -175,18 +291,8 @@
     maps = [step_map[0]]
     for b in range(1, blocks):
         maps.append(compose(maps[-1], step_map[b]))
-    state = entering(maps[-1])
-    later = mm("bhtk,bhjk->bhtj", reads[1:], jnp.stack(maps[:-1]))
-    reads = jnp.concatenate([reads[:1], later[..., :DK]])
-    adds = jnp.concatenate([adds[:1], adds[1:] + later[..., DK:]])
-    core = mm("bhtk,hvk->bhtv", reads, state) + adds
-    core = core.transpose(0, 2, 1, 3).reshape(seq_len, local_heads, DV)
-    core_half = core.astype(jnp.bfloat16)
-    core_back = lax.optimization_barrier(core_half).astype(jnp.float32)
-    gated = (
-        finish(core_back, gate_part.astype(jnp.float32), norm_gain)
-        .astype(jnp.bfloat16)
-        .reshape(seq_len, local_heads * DV)
+    gated = carried(
+        maps[-1], jnp.stack(maps[:-1]), reads, adds, flat, norm_gain.reshape(1, DV)
     )
     result = lax.all_to_all(gated, "head", split_axis=0, concat_axis=1, tiled=True)
     return result

time: 177 us -> 141 us (0.80)
  Pallas kernels: 0 us -> 62.5 us
  waiting for transfers between devices: 53.5 us -> 12.2 us
  matrix products: 45.6 us -> 22.1 us
  starting transfers between devices: 36 us -> 15.6 us
  local copies, waits for them, and re-layouts: 15 us -> 6.58 us
  blocking collectives: 14.3 us -> 11.6 us
    pallas_call x0 -> x1, Pallas kernels: none -> 62.5 us  [carried(): pl.pallas_call(carry_kernel, out_shape=jax.ShapeDtypeStruct((seq_len, hea...]
    all_to_all x3 -> x0, waiting for transfers between devices: 41.3 us -> none  [the longest x1 21 us: entering(): lax.all_to_all(pieces, 'ctx', 0, 0, axis_index_groups=along, tiled=True)]
    dot_general x33 -> x17, matrix products: 45.6 us -> 22.1 us  [mm(): return jnp.einsum(spec, a, b, precision=TOP_PRECISION)]
    all_to_all x3 -> x0, starting transfers between devices: 20.5 us -> none  [the longest x1 9.26 us: entering(): lax.all_to_all(pieces, 'ctx', 0, 0, axis_index_groups=along, tiled=True)]
    all_to_all x1, blocking collectives: 14.3 us -> 11.6 us  [body(): lax.all_to_all(gated, 'head', split_axis=0, concat_axis=1, tiled=True)]
    convert_element_type x3 -> x0, local copies, waits for them, and re-layouts: 2.57 us -> none  [the longest x1 2.34 us: body(): gate_part.astype(jnp.float32)]
    unnamed x27 -> x8, local copies, waits for them, and re-layouts: 3.9 us -> 1.58 us
    convert_element_type x2 -> x0, other arithmetic: 2.17 us -> none  [the longest x1 1.93 us: body(): gate_part.astype(jnp.float32)]
  transfers between devices with their start and end apart: 6 -> 3, of which waited for: 6 -> 3; matrix products, arithmetic and copies ran while one was open for 9% -> 4% of each run, Pallas kernels for 0% -> 0%
where the time goes in v2:
time: 141 us
  Pallas kernels  62.5 us (44%)
  matrix products  22.1 us (16%)
  starting transfers between devices  15.6 us (11%)
  waiting for transfers between devices  12.2 us (9%)
  blocking collectives  11.6 us (8%)
  other arithmetic  9.94 us (7%)
  local copies, waits for them, and re-layouts  6.58 us (5%)
    pallas_call x1, Pallas kernels, carried(): pl.pallas_call(carry_kernel, out_shape=jax.ShapeDtypeStruct((seq_len, hea...  62.5 us
    dot_general x17, matrix products, mm(): return jnp.einsum(spec, a, b, precision=TOP_PRECISION)  22.1 us
    all_to_all x1, blocking collectives, body(): lax.all_to_all(gated, 'head', split_axis=0, concat_axis=1, tiled=True)  11.6 us
    all_to_all x1, waiting for transfers between devices, body(): lax.all_to_all(projected, 'head', split_axis=1, concat_axis=0, tiled=True)  11.3 us
    all_to_all x1, starting transfers between devices, body(): lax.all_to_all(gate_logits, 'head', split_axis=1, concat_axis=0, tiled=True)  10.1 us
    all_to_all x1, starting transfers between devices, body(): lax.all_to_all(projected, 'head', split_axis=1, concat_axis=0, tiled=True)  4.21 us
  transfers between devices with their start and end apart: 3, of which 3 were waited for; matrix products, arithmetic and copies ran while one was open for 4% of the time, Pallas kernels for 0%

profile of v2, /device:TPU:1, one launch (start us, length us, event | category | flops | bytes accessed | tf_op | source)
XLA Modules:
  0.0 140.8 jit_solution(14554865634955870471)
XLA Ops:
  0.0 0.8 copy.41
  0.8 0.7 reshape.199
  1.5 10.1 %all-to-all-start = ((bf16[8,2,128]{2,1,0:T(2,128)(2,1)}), bf16[8,2,128]{2,1,0:T(2,128)(2,1)S(1)}, u32[]{:S(2)}, u32[]{:S(2)}) async-start(bf16[8,2,128]{2,1,0:T(2,128)(2,1)} %reshape.199), calls=%async_computation | async-start | bytes 8192 | tf_op jit(solution)/shard_map/all_to_all | solution.py:260
  11.7 0.7 exponential_negate_fusion
  12.3 0.7 convert_element_type.35
  13.4 2.1 %copy.102 = bf16[4,8,8,1536]{3,2,0,1:T(8,128)(2,1)} copy(bf16[4,8,8,1536]{3,2,1,0:T(8,128)(2,1)} %bitcast.90) | data formatting | bytes 1572864 | tf_op jit(solution)/shard_map/all_to_all | solution.py:259
  16.1 4.2 %all-to-all-start.1 = ((bf16[32,8,1536]{2,0,1:T(8,128)(2,1)}), bf16[32,8,1536]{2,0,1:T(8,128)(2,1)S(1)}, u32[]{:S(2)}, u32[]{:S(2)}) async-start(bf16[32,8,1536]{2,0,1:T(8,128)(2,1)} %bitcast.73), calls=%async_computation.1 | async-start | bytes 1572864 | tf_op jit(solution)/shard_map/all_to_all | solution.py:259
  21.2 11.3 %all-to-all-done.1 = bf16[32,8,1536]{2,0,1:T(8,128)(2,1)S(1)} async-done(((bf16[32,8,1536]{2,0,1:T(8,128)(2,1)}), bf16[32,8,1536]{2,0,1:T(8,128)(2,1)S(1)}, u32[]{:S(2)}, u32[]{:S(2)}) %all-to-all-start.1) | async-done | bytes 786464 | tf_op jit(solution)/shard_map/all_to_all | solution.py:259
  32.7 1.3 collective-permute-start
  35.3 1.9 %divide_multiply_fusion = f32[256,2,512]{2,1,0:T(2,128)S(1)} fusion(f32[259,2,512]{2,1,0:T(2,128)S(1)} %maximum_convert_fusion, f32[2,512]{1,0:T(2,128)S(1)} %mul.160, f32[2,512]{1,0:T(2,128)S(1)} %mul.157, f32[2,512]{1,0:T(2,128)S(1)} %mul.154, f32[2,512]{1,0:T(2,128)S(1)} %mul.151), kind=kLoop, calls=%fused_computation.11 | loop fusion | flops 2883584 | bytes 5259264 | tf_op jit(solution)/shard_map/jit(silu)/mul | solution.py:273
  37.2 0.6 multiply_reduce_fusion
  38.7 0.9 slice_multiply_fusion.6
  40.0 2.1 %fusion.3 = f32[16,128,64]{1,2,0:T(8,128)S(1)} fusion(f32[16,64,128]{2,1,0:T(8,128)S(1)} %bitcast.74, f32[16,64,128]{2,1,0:T(8,128)S(1)} %bitcast.78), kind=kOutput, calls=%fused_computation.19 | convolution fusion | flops 201588736 | bytes 1572864 | tf_op jit(solution)/shard_map/btk,bsk->bts/dot_general | solution.py:47
  42.1 1.4 fusion.24
  43.5 1.2 convolution_subtract_fusion.4
  44.7 1.2 fusion.22
  45.9 1.0 convolution_subtract_fusion.3
  46.9 1.2 fusion.20
  48.2 1.0 convolution_subtract_fusion.2
  49.2 1.2 fusion.18
  50.4 1.0 convolution_subtract_fusion.1
  51.4 1.2 fusion.16
  52.6 1.2 convolution_subtract_fusion
  54.1 1.1 fusion.7
  55.1 1.4 convolution_negate_fusion
  56.5 4.1 %multiply_subtract_fusion = f32[16,256,128]{2,1,0:T(8,128)S(1)} fusion(f32[16,64,256]{2,1,0:T(8,128)S(1)} %fusion.7, f32[256,128]{1,0:T(8,128)S(1)} %fusion.49, f32[16]{0:T(128)S(1)} %exp.46, f32[16,64,128]{2,1,0:T(8,128)S(1)} %bitcast.75, f32[16,64]{1,0:T(8,128)S(1)} %get-tuple-element.23), kind=kOutput, calls=%fused_computation | convolution fusion | flops 403832832 | bytes 3805248 | tf_op jit(solution)/shard_map/bsj,bsk->bjk/dot_general | solution.py:47
  62.6 1.2 fusion.79
  63.8 1.0 pad_maximum_fusion.1
  64.8 1.3 pad_maximum_fusion.maps
  66.0 62.5 %shard_map.64 = bf16[256,512]{1,0:T(8,128)(2,1)} custom-call(f32[8,192,128]{2,1,0:T(8,128)} %bitcast.81, f32[3,4,256,128]{3,2,1,0:T(8,128)} %pad_maximum_fusion.maps, f32[4,4,64,128]{3,2,1,0:T(8,128)} %bitcast.83, f32[4,4,64,128]{3,2,1,0:T(8,128)} %bitcast.82, bf16[256,1536]{1,0:T(8,128)(2,1)} %bitcast.77, f32[1,128]{1,0:T(1,128)} %bitcast.100), custom_call_target="tpu_custom_call" | custom-call | tf_op jit(solution)/shard_map/pallas_call | solution.py:234
  128.5 11.6 %all_to_all.51 = bf16[8,32,512]{2,1,0:T(8,128)(2,1)S(1)} all-to-all(bf16[8,32,512]{2,1,0:T(8,128)(2,1)} %bitcast.87), channel_id=1, replica_groups=mesh['ctx'=64,'head'=8] {'head'}, dimensions={0} | all-to-all | bytes 524288 | tf_op jit(solution)/shard_map/all_to_all | solution.py:297
  140.1 0.7 copy.98
  (62 shorter events, 6.7 us)
Async XLA Ops:
  0.0 20.7 %copy-start.1 = (f32[4]{0:T(128)S(1)}, f32[4]{0:T(128)}, u32[]{:S(2)}) copy-start(f32[4]{0:T(128)} %param.10) | copy-start | bytes 52
  1.5 14.6 %all-to-all-start = ((bf16[8,2,128]{2,1,0:T(2,128)(2,1)}), bf16[8,2,128]{2,1,0:T(2,128)(2,1)S(1)}, u32[]{:S(2)}, u32[]{:S(2)}) async-start(bf16[8,2,128]{2,1,0:T(2,128)(2,1)} %reshape.199), calls=%async_computation | async-start | bytes 8192 | tf_op jit(solution)/shard_map/all_to_all | solution.py:260
  16.1 16.4 %all-to-all-start.1 = ((bf16[32,8,1536]{2,0,1:T(8,128)(2,1)}), bf16[32,8,1536]{2,0,1:T(8,128)(2,1)S(1)}, u32[]{:S(2)}, u32[]{:S(2)}) async-start(bf16[32,8,1536]{2,0,1:T(8,128)(2,1)} %bitcast.73), calls=%async_computation.1 | async-start | bytes 1572864 | tf_op jit(solution)/shard_map/all_to_all | solution.py:259
  32.5 2.8 %copy-start = (bf16[32,8,1536]{2,0,1:T(8,128)(2,1)}, bf16[32,8,1536]{2,0,1:T(8,128)(2,1)S(1)}, u32[]{:S(2)}) copy-start(bf16[32,8,1536]{2,0,1:T(8,128)(2,1)S(1)} %all-to-all-done.1) | copy-start | bytes 2359300
  32.7 2.1 %collective-permute-start = (bf16[3,2,512]{2,1,0:T(2,128)(2,1)S(1)}, bf16[3,2,512]{2,1,0:T(2,128)(2,1)S(1)}, u32[]{:S(2)}, u32[]{:S(2)}) collective-permute-start(bf16[3,2,512]{2,1,0:T(2,128)(2,1)S(1)} %slice.142), channel_id=1, source_target_pairs={{0,8},{8,16},{16,24},{24,32},{32,40},{40,48},{48,56},{56,64},{64,7... | collective-permute-start | bytes 18440 | tf_op jit(solution)/shard_map/ppermute | solution.py:23

commit v3 on v2

v3 whole, which is shorter than its diff:
```python
import jax
import jax.numpy as jnp
from jax import lax
from jax.experimental import pallas as pl
from jax.experimental.pallas import tpu as pltpu
from jax.sharding import PartitionSpec as P

KEY_HEAD_COUNT = 16
HV = 32
DK = 128
DV = 128
CONV = 4
SPAN = 64


TOP_PRECISION = lax.Precision.HIGHEST
ROW = 8


def passed_along(array, axis, by):
    length = lax.axis_size(axis)
    pairs = [(i, i + by) for i in range(length) if 0 <= i + by < length]
    return lax.ppermute(array, axis, pairs)


def nn(a, b):
    return lax.dot_general(
        a, b, (((1,), (0,)), ((), ())),
        precision=TOP_PRECISION, preferred_element_type=jnp.float32,
    )


def nt(a, b):
    return lax.dot_general(
        a, b, (((1,), (1,)), ((), ())),
        precision=TOP_PRECISION, preferred_element_type=jnp.float32,
    )


def tn(a, b):
    return lax.dot_general(
        a, b, (((0,), (0,)), ((), ())),
        precision=TOP_PRECISION, preferred_element_type=jnp.float32,
    )


def iotas(rows, cols):
    return (
        lax.broadcasted_iota(jnp.int32, (rows, cols), 0),
        lax.broadcasted_iota(jnp.int32, (rows, cols), 1),
    )


def unit_inverses(lowers):
    n = lowers[0].shape[0]
    row, col = iotas(n, n)

    def joint(size):
        return (row // (2 * size) == col // (2 * size)) & (row // size != col // size)

    eye = (row == col).astype(jnp.float32)
    inverses = [eye - jnp.where(joint(1), low, 0.0) for low in lowers]
    size = 2
    while size < n:
        here = joint(size)
        inner = [nn(jnp.where(here, low, 0.0), inv) for low, inv in zip(lowers, inverses)]
        inverses = [inv - nn(inv, part) for inv, part in zip(inverses, inner)]
        size *= 2
    return inverses


def terms_kernel(
    arrived, edge, taps, columns, rows, pieces, maps, reads, adds, window, active, total
):
    blocks, heads = reads.shape[:2]
    ratio = HV // KEY_HEAD_COUNT
    key_heads = heads // ratio
    channels = (2 + ratio) * DK
    features = channels + ratio * DV
    seq_len = arrived.shape[0]
    pad = edge.shape[0]
    window[:pad, :] = edge[...].astype(jnp.float32)
    for j in range(key_heads):
        window[pad:, j * channels : (j + 1) * channels] = arrived[
            :, j * features : j * features + channels
        ].astype(jnp.float32)
    for b in range(blocks):
        for g in range(key_heads * channels // DK):
            at = slice(g * DK, (g + 1) * DK)
            low = b * SPAN + pad - CONV + 1
            mixed = taps[0:1, at] * window[low : low + SPAN, at]
            for i in range(1, CONV):
                mixed = mixed + taps[i : i + 1, at] * window[low + i : low + i + SPAN, at]
            mixed = jax.nn.silu(mixed)
            if g % (2 + ratio) < 2:
                mixed = mixed * lax.rsqrt(jnp.sum(mixed * mixed, axis=-1, keepdims=True) + 1e-06)
            active[b * SPAN : (b + 1) * SPAN, at] = mixed
    row, col = iotas(SPAN, SPAN)
    wide_row, wide_col = iotas(2 * DK, DK)
    eye = (wide_row == wide_col).astype(jnp.float32)
    for h in range(heads):
        total[h] = eye
    per = 2

    def block_terms(step, carry):
        items = [(step * per + p, h) for p in range(per) for h in range(heads)]
        keys, queries, values, both = [], [], [], []
        for p in range(per):
            at = pl.ds(pl.multiple_of((step * per + p) * SPAN, SPAN), SPAN)
            for j in range(key_heads):
                base = j * channels
                query = active[at, base : base + DK]
                key = active[at, base + DK : base + 2 * DK]
                product = nt(jnp.concatenate([key, query], axis=0), key)
                for i in range(ratio):
                    first = base + 2 * DK + i * DV
                    values.append(active[at, first : first + DV])
                    keys.append(key)
                    queries.append(query)
                    both.append(product)
        sums, steps, gaps, mixing = [], [], [], []
        for n, (b, h) in enumerate(items):
            pair = columns[b, h]
            sums.append(pair[:, 0:1])
            steps.append(pair[:, 1:2])
            gaps.append(jnp.exp(jnp.where(row >= col, sums[n] - rows[b, h], 0.0)))
            mixing.append(jnp.where(row > col, steps[n] * both[n][:SPAN] * gaps[n], 0.0))
        inverses = unit_inverses(mixing)
        solved = []
        for n in range(len(items)):
            grown = jnp.exp(sums[n])
            target = jnp.concatenate([steps[n] * grown * keys[n], -steps[n] * values[n]], axis=1)
            solved.append(nn(inverses[n], target))
        for n, (b, h) in enumerate(items):
            end = rows[b, h][:, SPAN - 1 : SPAN]
            last = jnp.exp(end - sums[n]) * keys[n]
            change = jnp.exp(end) * eye - tn(solved[n], last)
            score = jnp.where(row >= col, both[n][SPAN:] * gaps[n], 0.0)
            read = nn(score, solved[n])
            reads[b, h] = jnp.exp(sums[n]) * queries[n] - read[:, :DK]
            adds[b, h] = -read[:, DK:]
            product = nn(total[h], change[:DK])
            total[h, :DK, :] = product[:DK]
            total[h, DK:, :] = product[DK:] + change[DK:]
            maps[b, h] = total[h]
        return carry

    lax.fori_loop(0, blocks // per, block_terms, 0)
    width = pieces.shape[1] - DK
    for piece in range(ROW):
        h, part = piece % heads, piece // heads
        pieces[piece, :DK, :] = total[h, :DK, :]
        pieces[piece, DK:, :] = total[h, DK + part * width : DK + (part + 1) * width, :]


def local_terms(arrived, edge, taps, columns, rows):
    blocks, heads = columns.shape[:2]
    seq_len = arrived.shape[0]
    width = DV * heads // ROW
    channels = taps.shape[1]
    vmem = pl.BlockSpec(memory_space=pltpu.VMEM)
    return pl.pallas_call(
        terms_kernel,
        out_shape=[
            jax.ShapeDtypeStruct((ROW, DK + width, DK), jnp.float32),
            jax.ShapeDtypeStruct((blocks, heads, 2 * DK, DK), jnp.float32),
            jax.ShapeDtypeStruct((blocks, heads, SPAN, DK), jnp.float32),
            jax.ShapeDtypeStruct((blocks, heads, SPAN, DV), jnp.float32),
        ],
        in_specs=[vmem] * 5,
        out_specs=[vmem] * 4,
        scratch_shapes=[
            pltpu.VMEM((seq_len + edge.shape[0], channels), jnp.float32),
            pltpu.VMEM((seq_len, channels), jnp.float32),
            pltpu.VMEM((heads, 2 * DK, DK), jnp.float32),
        ],
    )(arrived, edge, taps, columns, rows)


OFFSETS = (4, 3, 5, 2, 6, 1, 7)


def carry_kernel(
    pieces, maps, reads, adds, arrived, gain, out,
    got, prefix, row_total, row_maps, states, entered, core_reads, core_adds, gated, landed,
    send_a, recv_a, send_b, recv_b, send_c, recv_c, send_d, recv_d,
):
    blocks, heads = reads.shape[:2]
    count = ROW
    mine = lax.axis_index("ctx")
    r, z = mine // count, lax.rem(mine, count)

    def in_row(k):
        return r * count + lax.rem(z + k, count)

    def in_column(k):
        return lax.rem(r + k, count) * count + z

    barrier = pltpu.get_barrier_semaphore()
    for k in range(1, count):
        for peer in (in_row(k), in_column(k)):
            pl.semaphore_signal(
                barrier, inc=1, device_id={"ctx": peer}, device_id_type=pl.DeviceIdType.MESH
            )
    groups = lax.axis_size("head")
    group = lax.axis_index("head")
    for k in range(1, groups):
        pl.semaphore_signal(
            barrier, inc=1, device_id={"head": lax.rem(group + k, groups)},
            device_id_type=pl.DeviceIdType.MESH,
        )
    pl.semaphore_wait(barrier, 2 * (count - 1) + groups - 1)

    def send(source, target, send_sem, recv_sem, peer, axis="ctx"):
        copy = pltpu.make_async_remote_copy(
            src_ref=source, dst_ref=target, send_sem=send_sem, recv_sem=recv_sem,
            device_id={axis: peer}, device_id_type=pl.DeviceIdType.MESH,
        )
        copy.start()
        return copy

    first = [
        send(
            pieces.at[lax.rem(z + k, count)], got.at[z],
            send_a.at[k], recv_a.at[k], in_row(k),
        )
        for k in OFFSETS
    ]
    got[z] = pieces[z]

    def affine(i, carry):
        b, h = i // heads, lax.rem(i, heads)
        both = nt(reads[b + 1, h], maps[b, h])
        at = pl.ds(pl.multiple_of((b + 1) * SPAN, SPAN), SPAN)
        core_reads[h, at, :] = both[:, :DK]
        core_adds[h, at, :] = both[:, DK:] + adds[b + 1, h]
        return carry

    lax.fori_loop(0, (blocks - 1) * heads, affine, 0)
    for h in range(heads):
        core_reads[h, :SPAN, :] = reads[0, h]
        core_adds[h, :SPAN, :] = adds[0, h]

    for copy in first:
        copy.wait()
    prefix[1] = got[0]

    def advance(c, carry):
        product = nn(prefix[c], got[c, :DK, :])
        prefix[c + 1, :DK, :] = product[:DK]
        prefix[c + 1, DK:, :] = product[DK:] + got[c, DK:, :]
        return carry

    lax.fori_loop(1, count - 1, advance, 0)
    product = nn(prefix[count - 1], got[count - 1, :DK, :])
    row_total[:DK, :] = product[:DK]
    row_total[DK:, :] = product[DK:] + got[count - 1, DK:, :]
    second = [
        send(row_total, row_maps.at[r], send_b.at[k], recv_b.at[k], in_column(k))
        for k in OFFSETS
    ]
    row_maps[r] = row_total[...]
    for copy in second:
        copy.wait()
    state = jnp.where(r > 0, row_maps[0, DK:, :], 0.0)
    for c in range(1, count - 1):
        longer = nn(state, row_maps[c, :DK, :]) + row_maps[c, DK:, :]
        state = jnp.where(c < r, longer, state)
    states[0] = state
    for c in range(1, count):
        states[c] = nn(state, prefix[c, :DK, :]) + prefix[c, DK:, :]
    third = [
        send(
            states.at[lax.rem(z + k, count)], entered.at[z],
            send_c.at[k], recv_c.at[k], in_row(k),
        )
        for k in OFFSETS
    ]
    entered[z] = states[z]
    for copy in third:
        copy.wait()
    features = arrived.shape[1] // heads
    for h in range(heads):
        entering = jnp.concatenate([entered[h + heads * p] for p in range(count // heads)], axis=0)
        core = nt(core_reads[h], entering) + core_adds[h]
        core = core.astype(jnp.bfloat16).astype(jnp.float32)
        at = (h // 2) * 2 * features + 2 * DK + 2 * DV + (h % 2) * DV
        gate = arrived[:, at : at + DV].astype(jnp.float32)
        scale = lax.rsqrt(jnp.mean(core * core, axis=-1, keepdims=True) + 1e-06)
        normed = core * scale * gain[...]
        gated[:, h * DV : (h + 1) * DV] = (normed * jax.nn.silu(gate)).astype(jnp.bfloat16)
    kept = out.shape[0]

    def tokens_of(owner):
        return gated.at[pl.ds(pl.multiple_of(owner * kept, kept), kept), :]

    fourth = []
    for k in range(1, groups):
        peer = lax.rem(group + k, groups)
        fourth.append(
            send(tokens_of(peer), landed.at[group], send_d.at[k], recv_d.at[k], peer, "head")
        )
    landed[group] = tokens_of(group)[...]
    for copy in fourth:
        copy.wait()
    for g in range(groups):
        out[:, g * heads * DV : (g + 1) * heads * DV] = landed[g]


def carried(pieces, maps, reads, adds, arrived, gain):
    blocks, heads = reads.shape[:2]
    seq_len = arrived.shape[0]
    groups = lax.axis_size("head")
    width = pieces.shape[1] - DK
    piece = (ROW, DK + width, DK)
    half = (ROW, width, DK)
    full = (heads, seq_len, DK)
    vmem = pl.BlockSpec(memory_space=pltpu.VMEM)
    return pl.pallas_call(
        carry_kernel,
        out_shape=jax.ShapeDtypeStruct((seq_len // groups, groups * heads * DV), jnp.bfloat16),
        in_specs=[vmem] * 6,
        out_specs=vmem,
        scratch_shapes=[
            pltpu.VMEM(piece, jnp.float32),
            pltpu.VMEM(piece, jnp.float32),
            pltpu.VMEM(piece[1:], jnp.float32),
            pltpu.VMEM(piece, jnp.float32),
            pltpu.VMEM(half, jnp.float32),
            pltpu.VMEM(half, jnp.float32),
            pltpu.VMEM(full, jnp.float32),
            pltpu.VMEM(full, jnp.float32),
            pltpu.VMEM((seq_len, heads * DV), jnp.bfloat16),
            pltpu.VMEM((groups, seq_len // groups, heads * DV), jnp.bfloat16),
        ]
        + [pltpu.SemaphoreType.DMA((ROW,))] * 6
        + [pltpu.SemaphoreType.DMA((groups,))] * 2,
        compiler_params=pltpu.CompilerParams(collective_id=0, has_side_effects=True),
    )(pieces, maps, reads, adds, arrived, gain)


def body(projected, gate_logits, conv_weight, decay_log, step_bias, norm_gain):
    ratio = HV // KEY_HEAD_COUNT
    channels = (2 + ratio) * DK
    features = channels + ratio * DV
    logits = lax.all_to_all(gate_logits, "head", split_axis=1, concat_axis=0, tiled=True)
    arrived = lax.all_to_all(projected, "head", split_axis=1, concat_axis=0, tiled=True)
    seq_len = arrived.shape[0]
    local_keys = arrived.shape[1] // features
    heads = local_keys * ratio
    blocks = seq_len // SPAN
    logits = logits.astype(jnp.float32).reshape(seq_len, local_keys, 2, ratio)
    step_size = jax.nn.sigmoid(logits[:, :, 0].reshape(seq_len, heads))
    decays = -jnp.exp(decay_log) * jax.nn.softplus(
        logits[:, :, 1].reshape(seq_len, heads) + step_bias
    )
    sums = jnp.cumsum(decays.reshape(blocks, SPAN, heads), axis=1).transpose(0, 2, 1)
    steps = step_size.reshape(blocks, SPAN, heads).transpose(0, 2, 1)
    columns = jnp.stack([sums, steps], axis=-1)
    tail = arrived[seq_len - CONV + 1 :].reshape(CONV - 1, local_keys, features)[:, :, :channels]
    edge = passed_along(tail.reshape(CONV - 1, local_keys * channels), "ctx", 1)
    edge = jnp.concatenate([jnp.zeros((8 - CONV + 1, edge.shape[1]), edge.dtype), edge])
    pieces, maps, reads, adds = local_terms(
        arrived, edge, conv_weight.astype(jnp.float32), columns, sums[:, :, None, :]
    )
    return carried(pieces, maps, reads, adds, arrived, norm_gain.reshape(1, DV))


def solution(mesh):
    return jax.shard_map(
        body,
        mesh=mesh,
        in_specs=(
            P(("ctx", "head"), None),
            P(("ctx", "head"), None),
            P(None, "head"),
            P("head"),
            P("head"),
            P(),
        ),
        out_specs=P(("ctx", "head"), None),
        check_vma=False,
    )
```

time: 141 us -> 122 us (0.87)
  matrix products: 22.1 us -> 0 us
  Pallas kernels: 62.5 us -> 84.1 us
  blocking collectives: 11.6 us -> 0 us
  other arithmetic: 9.94 us -> 0.86 us
    dot_general x17 -> x0, matrix products: 22.1 us -> none  [mm(): return jnp.einsum(spec, a, b, precision=TOP_PRECISION)]
    pallas_call x1 -> x2, Pallas kernels: 62.5 us -> 84.1 us  [the longest x1 68.8 us: carried(): pl.pallas_call(carry_kernel, out_shape=jax.ShapeDtypeStruct((seq_len // g...]
    all_to_all x1 -> x0, blocking collectives: 11.6 us -> none  [body(): lax.all_to_all(gated, 'head', split_axis=0, concat_axis=1, tiled=True)]
    mul x4 -> x1, other arithmetic: 3.2 us -> 0.09 us  [body(): -jnp.exp(decay_log)]
    all_to_all x1, waiting for transfers between devices: 0.61 us -> 2.47 us  [body(): lax.all_to_all(gate_logits, 'head', split_axis=1, concat_axis=0, tiled=True)]
    unnamed x8 -> x17, local copies, waits for them, and re-layouts: 1.58 us -> 3.3 us
  transfers between devices with their start and end apart: 3 -> 3, of which waited for: 3 -> 2; matrix products, arithmetic and copies ran while one was open for 4% -> 4% of each run, Pallas kernels for 0% -> 0%
where the time goes in v3:
time: 122 us; the launch traced here: 121 us
  Pallas kernels  84.1 us (69%)
  starting transfers between devices  15.5 us (13%)
  waiting for transfers between devices  13.2 us (11%)
  local copies, waits for them, and re-layouts  7.56 us (6%)
    pallas_call x1, Pallas kernels, carried(): pl.pallas_call(carry_kernel, out_shape=jax.ShapeDtypeStruct((seq_len // g...  68.8 us
    pallas_call x1, Pallas kernels, local_terms(): pl.pallas_call(terms_kernel, out_shape=[jax.ShapeDtypeStruct((ROW, DK + w...  15.3 us
    all_to_all x1, waiting for transfers between devices, body(): lax.all_to_all(projected, 'head', split_axis=1, concat_axis=0, tiled=True)  10.7 us
    all_to_all x1, starting transfers between devices, body(): lax.all_to_all(gate_logits, 'head', split_axis=1, concat_axis=0, tiled=True)  10.1 us
    all_to_all x1, starting transfers between devices, body(): lax.all_to_all(projected, 'head', split_axis=1, concat_axis=0, tiled=True)  4.14 us
    unnamed x17, local copies, waits for them, and re-layouts  3.3 us
    all_to_all x1, waiting for transfers between devices, body(): lax.all_to_all(gate_logits, 'head', split_axis=1, concat_axis=0, tiled=True)  2.47 us
  transfers between devices with their start and end apart: 3, of which 2 were waited for; matrix products, arithmetic and copies ran while one was open for 4% of the time, Pallas kernels for 0%

profile of v3, /device:TPU:1, one launch (start us, length us, event | category | flops | bytes accessed | tf_op | source)
XLA Modules:
  0.0 121.3 jit_solution(17993234832002217494)
XLA Ops:
  0.0 0.0 copy-start.2
  0.0 0.0 copy-start.3
  0.0 0.8 copy.11
  0.8 0.7 reshape.45
  1.5 10.1 %all-to-all-start.1 = ((bf16[8,2,128]{2,1,0:T(2,128)(2,1)}), bf16[8,2,128]{2,1,0:T(2,128)(2,1)S(1)}, u32[]{:S(2)}, u32[]{:S(2)}) async-start(bf16[8,2,128]{2,1,0:T(2,128)(2,1)} %reshape.45), calls=%async_computation.1 | async-start | bytes 8192 | tf_op jit(solution)/shard_map/all_to_all | solution.py:346
  11.6 2.1 %copy.21 = bf16[4,8,8,1536]{3,2,0,1:T(8,128)(2,1)} copy(bf16[4,8,8,1536]{3,2,1,0:T(8,128)(2,1)} %bitcast.38) | data formatting | bytes 1572864 | tf_op jit(solution)/shard_map/all_to_all | solution.py:347
  13.7 2.5 %all-to-all-done.1 = bf16[8,2,128]{2,1,0:T(2,128)(2,1)S(1)} async-done(((bf16[8,2,128]{2,1,0:T(2,128)(2,1)}), bf16[8,2,128]{2,1,0:T(2,128)(2,1)S(1)}, u32[]{:S(2)}, u32[]{:S(2)}) %all-to-all-start.1) | async-done | bytes 4128 | tf_op jit(solution)/shard_map/all_to_all | solution.py:346
  16.1 4.1 %all-to-all-start = ((bf16[32,8,1536]{2,0,1:T(8,128)(2,1)}), bf16[32,8,1536]{2,0,1:T(8,128)(2,1)S(1)}, u32[]{:S(2)}, u32[]{:S(2)}) async-start(bf16[32,8,1536]{2,0,1:T(8,128)(2,1)} %bitcast.33), calls=%async_computation | async-start | bytes 1572864 | tf_op jit(solution)/shard_map/all_to_all | solution.py:347
  20.3 0.0 copy-done.4
  20.3 0.0 copy-done.2
  20.3 0.6 convert_element_type.13.taps
  20.9 0.1 reshape.46
  21.0 0.1 reshape.44
  21.1 0.1 reshape_squeeze.4
  21.2 0.1 div.8
  21.3 0.0 copy-done.3
  21.3 0.1 fusion
  21.4 0.1 copy.13
  21.5 0.1 reduce_window_sum.11
  21.6 0.1 copy.14
  21.7 0.0 copy-start.1
  21.7 10.7 %all-to-all-done = bf16[32,8,1536]{2,0,1:T(8,128)(2,1)S(1)} async-done(((bf16[32,8,1536]{2,0,1:T(8,128)(2,1)}), bf16[32,8,1536]{2,0,1:T(8,128)(2,1)S(1)}, u32[]{:S(2)}, u32[]{:S(2)}) %all-to-all-start) | async-done | bytes 786464 | tf_op jit(solution)/shard_map/all_to_all | solution.py:347
  32.5 0.0 copy-start
  32.5 1.3 %collective-permute-start = (bf16[3,1024]{1,0:T(4,128)(2,1)S(1)}, bf16[3,1024]{1,0:T(4,128)(2,1)S(1)}, u32[]{:S(2)}, u32[]{:S(2)}) collective-permute-start(bf16[3,1024]{1,0:T(4,128)(2,1)S(1)} %bitcast.42), channel_id=1, source_target_pairs={{0,8},{8,16},{16,24},{24,32},{32,40},{40,48},{48,56},{56,64},{64,7... | collective-permute-start | bytes 18440 | tf_op jit(solution)/shard_map/ppermute | solution.py:23
  33.8 1.0 copy.16.columns
  34.9 0.0 collective-permute-done
  34.9 0.6 concatenate.3.edge
  35.5 0.0 copy-done.1
  35.5 0.0 copy-done
  35.5 15.3 %shard_map.64 = (f32[8,192,128]{2,1,0:T(8,128)}, f32[4,4,256,128]{3,2,1,0:T(8,128)}, f32[4,4,64,128]{3,2,1,0:T(8,128)}, f32[4,4,64,128]{3,2,1,0:T(8,128)}) custom-call(bf16[256,1536]{1,0:T(8,128)(2,1)} %bitcast.36, bf16[8,1024]{1,0:T(8,128)(2,1)} %concatenate.3.edge, f32[4,1024]{1,0:T(4,128)} %convert_element_type.13.taps, f32[4,4,64,2]{3,2,1,0:T(8,128)} %copy.16.columns, ...), custom_call_target="tpu_custom_call" | custom-call | tf_op jit(solution)/shard_map/pallas_call | solution.py:162
  50.9 68.8 %shard_map.65 = bf16[32,4096]{1,0:T(8,128)(2,1)} custom-call(f32[8,192,128]{2,1,0:T(8,128)} %get-tuple-element.9.pieces, f32[4,4,256,128]{3,2,1,0:T(8,128)} %get-tuple-element.10.maps, f32[4,4,64,128]{3,2,1,0:T(8,128)} %get-tuple-element.11.reads, f32[4,4,64,128]{3,2,1,0:T(8,128)} %get-tuple-element.12.adds, bf16[256,1536]{1,0:T(8,128)(2,1)} %bitcast.37, ...), custom_call_target="tpu_custom_call" | custom-call | tf_op jit(solution)/shard_map/pallas_call | solution.py:319
  119.7 1.7 %copy.24 = bf16[32,4096]{1,0:T(8,128)(2,1)} copy(bf16[32,4096]{1,0:T(8,128)(2,1)} %shard_map.65) | data formatting | bytes 524288
  (12 shorter events, 0.1 us)
Async XLA Ops:
  0.0 20.3 %copy-start.4 = (f32[4]{0:T(128)S(1)}, f32[4]{0:T(128)}, u32[]{:S(2)}) copy-start(f32[4]{0:T(128)} %param.9) | copy-start | bytes 52
  0.0 20.3 %copy-start.2 = (bf16[4,1024]{1,0:T(4,128)(2,1)S(1)}, bf16[4,1024]{1,0:T(4,128)(2,1)}, u32[]{:S(2)}) copy-start(bf16[4,1024]{1,0:T(4,128)(2,1)} %param.8) | copy-start | bytes 24580
  0.0 21.3 %copy-start.3 = (f32[4]{0:T(128)S(1)}, f32[4]{0:T(128)}, u32[]{:S(2)}) copy-start(f32[4]{0:T(128)} %param.10) | copy-start | bytes 52
  1.5 14.6 %all-to-all-start.1 = ((bf16[8,2,128]{2,1,0:T(2,128)(2,1)}), bf16[8,2,128]{2,1,0:T(2,128)(2,1)S(1)}, u32[]{:S(2)}, u32[]{:S(2)}) async-start(bf16[8,2,128]{2,1,0:T(2,128)(2,1)} %reshape.45), calls=%async_computation.1 | async-start | bytes 8192 | tf_op jit(solution)/shard_map/all_to_all | solution.py:346
  16.1 16.3 %all-to-all-start = ((bf16[32,8,1536]{2,0,1:T(8,128)(2,1)}), bf16[32,8,1536]{2,0,1:T(8,128)(2,1)S(1)}, u32[]{:S(2)}, u32[]{:S(2)}) async-start(bf16[32,8,1536]{2,0,1:T(8,128)(2,1)} %bitcast.33), calls=%async_computation | async-start | bytes 1572864 | tf_op jit(solution)/shard_map/all_to_all | solution.py:347
  21.7 13.8 %copy-start.1 = (f32[4,64,4]{1,2,0:T(4,128)}, f32[4,64,4]{1,2,0:T(4,128)S(1)}, u32[]{:S(2)}) copy-start(f32[4,64,4]{1,2,0:T(4,128)S(1)} %copy.14) | copy-start | bytes 12292
  32.5 3.1 %copy-start = (bf16[32,8,1536]{2,0,1:T(8,128)(2,1)}, bf16[32,8,1536]{2,0,1:T(8,128)(2,1)S(1)}, u32[]{:S(2)}) copy-start(bf16[32,8,1536]{2,0,1:T(8,128)(2,1)S(1)} %all-to-all-done) | copy-start | bytes 2359300
  32.5 2.4 %collective-permute-start = (bf16[3,1024]{1,0:T(4,128)(2,1)S(1)}, bf16[3,1024]{1,0:T(4,128)(2,1)S(1)}, u32[]{:S(2)}, u32[]{:S(2)}) collective-permute-start(bf16[3,1024]{1,0:T(4,128)(2,1)S(1)} %bitcast.42), channel_id=1, source_target_pairs={{0,8},{8,16},{16,24},{24,32},{32,40},{40,48},{48,56},{56,64},{64,7... | collective-permute-start | bytes 18440 | tf_op jit(solution)/shard_map/ppermute | solution.py:23

commit v4 on v3

--- a/solution.py
+++ b/solution.py
@@ -100,7 +100,7 @@
     eye = (wide_row == wide_col).astype(jnp.float32)
     for h in range(heads):
         total[h] = eye
-    per = 2
+    per = 4
 
     def block_terms(step, carry):
         items = [(step * per + p, h) for p in range(per) for h in range(heads)]

time: 122 us -> 121 us (level)
  no operation moved by 1% of the time
where the time goes in v4:
time: 121 us
  Pallas kernels  83.3 us (69%)
  starting transfers between devices  15.5 us (13%)
  waiting for transfers between devices  13.2 us (11%)
  local copies, waits for them, and re-layouts  7.56 us (6%)
    pallas_call x1, Pallas kernels, carried(): pl.pallas_call(carry_kernel, out_shape=jax.ShapeDtypeStruct((seq_len // g...  68.8 us
    pallas_call x1, Pallas kernels, local_terms(): pl.pallas_call(terms_kernel, out_shape=[jax.ShapeDtypeStruct((ROW, DK + w...  14.6 us
    all_to_all x1, waiting for transfers between devices, body(): lax.all_to_all(projected, 'head', split_axis=1, concat_axis=0, tiled=True)  10.7 us
    all_to_all x1, starting transfers between devices, body(): lax.all_to_all(gate_logits, 'head', split_axis=1, concat_axis=0, tiled=True)  10.1 us
    all_to_all x1, starting transfers between devices, body(): lax.all_to_all(projected, 'head', split_axis=1, concat_axis=0, tiled=True)  4.14 us
    unnamed x17, local copies, waits for them, and re-layouts  3.3 us
    all_to_all x1, waiting for transfers between devices, body(): lax.all_to_all(gate_logits, 'head', split_axis=1, concat_axis=0, tiled=True)  2.47 us
  transfers between devices with their start and end apart: 3, of which 2 were waited for; matrix products, arithmetic and copies ran while one was open for 4% of the time, Pallas kernels for 0%

profile of v4, /device:TPU:1, one launch (start us, length us, event | category | flops | bytes accessed | tf_op | source)
XLA Modules:
  0.0 120.5 jit_solution(12339228011037101107)
XLA Ops:
  0.0 0.0 copy-start.4
  0.0 0.0 copy-start.2
  0.0 0.0 copy-start.3
  0.0 0.8 copy.11
  0.8 0.7 reshape.45
  1.5 10.1 %all-to-all-start.1 = ((bf16[8,2,128]{2,1,0:T(2,128)(2,1)}), bf16[8,2,128]{2,1,0:T(2,128)(2,1)S(1)}, u32[]{:S(2)}, u32[]{:S(2)}) async-start(bf16[8,2,128]{2,1,0:T(2,128)(2,1)} %reshape.45), calls=%async_computation.1 | async-start | bytes 8192 | tf_op jit(solution)/shard_map/all_to_all | solution.py:346
  11.6 2.1 %copy.21 = bf16[4,8,8,1536]{3,2,0,1:T(8,128)(2,1)} copy(bf16[4,8,8,1536]{3,2,1,0:T(8,128)(2,1)} %bitcast.38) | data formatting | bytes 1572864 | tf_op jit(solution)/shard_map/all_to_all | solution.py:347
  13.7 2.5 %all-to-all-done.1 = bf16[8,2,128]{2,1,0:T(2,128)(2,1)S(1)} async-done(((bf16[8,2,128]{2,1,0:T(2,128)(2,1)}), bf16[8,2,128]{2,1,0:T(2,128)(2,1)S(1)}, u32[]{:S(2)}, u32[]{:S(2)}) %all-to-all-start.1) | async-done | bytes 4128 | tf_op jit(solution)/shard_map/all_to_all | solution.py:346
  16.1 4.1 %all-to-all-start = ((bf16[32,8,1536]{2,0,1:T(8,128)(2,1)}), bf16[32,8,1536]{2,0,1:T(8,128)(2,1)S(1)}, u32[]{:S(2)}, u32[]{:S(2)}) async-start(bf16[32,8,1536]{2,0,1:T(8,128)(2,1)} %bitcast.33), calls=%async_computation | async-start | bytes 1572864 | tf_op jit(solution)/shard_map/all_to_all | solution.py:347
  20.3 0.0 copy-done.4
  20.3 0.0 copy-done.2
  20.3 0.6 convert_element_type.13.taps
  20.9 0.1 reshape.46
  21.0 0.1 reshape.44
  21.1 0.1 reshape_squeeze.4
  21.2 0.1 div.8
  21.3 0.0 copy-done.3
  21.3 0.1 fusion
  21.4 0.1 copy.13
  21.5 0.1 reduce_window_sum.11
  21.6 0.1 copy.14
  21.7 0.0 copy-start.1
  21.7 10.7 %all-to-all-done = bf16[32,8,1536]{2,0,1:T(8,128)(2,1)S(1)} async-done(((bf16[32,8,1536]{2,0,1:T(8,128)(2,1)}), bf16[32,8,1536]{2,0,1:T(8,128)(2,1)S(1)}, u32[]{:S(2)}, u32[]{:S(2)}) %all-to-all-start) | async-done | bytes 786464 | tf_op jit(solution)/shard_map/all_to_all | solution.py:347
  32.5 1.3 %collective-permute-start = (bf16[3,1024]{1,0:T(4,128)(2,1)S(1)}, bf16[3,1024]{1,0:T(4,128)(2,1)S(1)}, u32[]{:S(2)}, u32[]{:S(2)}) collective-permute-start(bf16[3,1024]{1,0:T(4,128)(2,1)S(1)} %bitcast.42), channel_id=1, source_target_pairs={{0,8},{8,16},{16,24},{24,32},{32,40},{40,48},{48,56},{56,64},{64,7... | collective-permute-start | bytes 18440 | tf_op jit(solution)/shard_map/ppermute | solution.py:23
  33.8 1.0 copy.16.columns
  34.9 0.0 collective-permute-done
  34.9 0.6 concatenate.3.edge
  35.5 0.0 copy-done.1
  35.5 0.0 copy-done
  35.5 14.6 %shard_map.64 = (f32[8,192,128]{2,1,0:T(8,128)}, f32[4,4,256,128]{3,2,1,0:T(8,128)}, f32[4,4,64,128]{3,2,1,0:T(8,128)}, f32[4,4,64,128]{3,2,1,0:T(8,128)}) custom-call(bf16[256,1536]{1,0:T(8,128)(2,1)} %bitcast.36, bf16[8,1024]{1,0:T(8,128)(2,1)} %concatenate.3.edge, f32[4,1024]{1,0:T(4,128)} %convert_element_type.13.taps, f32[4,4,64,2]{3,2,1,0:T(8,128)} %copy.16.columns, ...), custom_call_target="tpu_custom_call" | custom-call | tf_op jit(solution)/shard_map/pallas_call | solution.py:162
  50.1 68.8 %shard_map.65 = bf16[32,4096]{1,0:T(8,128)(2,1)} custom-call(f32[8,192,128]{2,1,0:T(8,128)} %get-tuple-element.9.pieces, f32[4,4,256,128]{3,2,1,0:T(8,128)} %get-tuple-element.10.maps, f32[4,4,64,128]{3,2,1,0:T(8,128)} %get-tuple-element.11.reads, f32[4,4,64,128]{3,2,1,0:T(8,128)} %get-tuple-element.12.adds, bf16[256,1536]{1,0:T(8,128)(2,1)} %bitcast.37, ...), custom_call_target="tpu_custom_call" | custom-call | tf_op jit(solution)/shard_map/pallas_call | solution.py:319
  118.9 1.7 %copy.24 = bf16[32,4096]{1,0:T(8,128)(2,1)} copy(bf16[32,4096]{1,0:T(8,128)(2,1)} %shard_map.65) | data formatting | bytes 524288
  (12 shorter events, 0.1 us)
Async XLA Ops:
  0.0 20.3 %copy-start.4 = (f32[4]{0:T(128)S(1)}, f32[4]{0:T(128)}, u32[]{:S(2)}) copy-start(f32[4]{0:T(128)} %param.9) | copy-start | bytes 52
  0.0 20.3 %copy-start.2 = (bf16[4,1024]{1,0:T(4,128)(2,1)S(1)}, bf16[4,1024]{1,0:T(4,128)(2,1)}, u32[]{:S(2)}) copy-start(bf16[4,1024]{1,0:T(4,128)(2,1)} %param.8) | copy-start | bytes 24580
  0.0 21.3 %copy-start.3 = (f32[4]{0:T(128)S(1)}, f32[4]{0:T(128)}, u32[]{:S(2)}) copy-start(f32[4]{0:T(128)} %param.10) | copy-start | bytes 52
  1.5 14.6 %all-to-all-start.1 = ((bf16[8,2,128]{2,1,0:T(2,128)(2,1)}), bf16[8,2,128]{2,1,0:T(2,128)(2,1)S(1)}, u32[]{:S(2)}, u32[]{:S(2)}) async-start(bf16[8,2,128]{2,1,0:T(2,128)(2,1)} %reshape.45), calls=%async_computation.1 | async-start | bytes 8192 | tf_op jit(solution)/shard_map/all_to_all | solution.py:346
  16.1 16.3 %all-to-all-start = ((bf16[32,8,1536]{2,0,1:T(8,128)(2,1)}), bf16[32,8,1536]{2,0,1:T(8,128)(2,1)S(1)}, u32[]{:S(2)}, u32[]{:S(2)}) async-start(bf16[32,8,1536]{2,0,1:T(8,128)(2,1)} %bitcast.33), calls=%async_computation | async-start | bytes 1572864 | tf_op jit(solution)/shard_map/all_to_all | solution.py:347
  21.7 13.8 %copy-start.1 = (f32[4,64,4]{1,2,0:T(4,128)}, f32[4,64,4]{1,2,0:T(4,128)S(1)}, u32[]{:S(2)}) copy-start(f32[4,64,4]{1,2,0:T(4,128)S(1)} %copy.14) | copy-start | bytes 12292
  32.5 3.1 %copy-start = (bf16[32,8,1536]{2,0,1:T(8,128)(2,1)}, bf16[32,8,1536]{2,0,1:T(8,128)(2,1)S(1)}, u32[]{:S(2)}) copy-start(bf16[32,8,1536]{2,0,1:T(8,128)(2,1)S(1)} %all-to-all-done) | copy-start | bytes 2359300
  32.5 2.4 %collective-permute-start = (bf16[3,1024]{1,0:T(4,128)(2,1)S(1)}, bf16[3,1024]{1,0:T(4,128)(2,1)S(1)}, u32[]{:S(2)}, u32[]{:S(2)}) collective-permute-start(bf16[3,1024]{1,0:T(4,128)(2,1)S(1)} %bitcast.42), channel_id=1, source_target_pairs={{0,8},{8,16},{16,24},{24,32},{32,40},{40,48},{48,56},{56,64},{64,7... | collective-permute-start | bytes 18440 | tf_op jit(solution)/shard_map/ppermute | solution.py:23
